TPU v7x, 32 devices: a whole 2x2x4 slice. The times are simulated.
32 devices in a mesh: dev: 32 (over z, y, x, core).
Axes of the slice: x: 2, y: 2, z: 4, core: 2. Of those that a mesh axis runs over, the one named last changes fastest.
Arguments:
- features: bfloat16 [16384, 1024], P('dev'), may hold values from -6 to 6
- w_hidden: bfloat16 [1024, 512], replicated, may hold values from -0.1875 to 0.1875
- w_out: bfloat16 [512, 128], replicated, may hold values from -0.25 to 0.25
- items: bfloat16 [65536, 128], P('dev'), may hold values from -200 to 200
- routes: int32 [16384, 4], P('dev'), may hold values from 0 to 511, all different within a row; in each aligned block of 512 rows (0 to 511, 512 to 1023, ...) at most 8 rows name the same one
- cluster_slot: int32 [512], replicated, may hold values from 0 to 511, each once
- sample_ids: int32 [512, 4096], P('dev'), may hold values from 0 to 127
- sample_counts: int32 [512, 4096], P('dev'), may hold values from 1 to 4095
- positives: int32 [16384, 4], P('dev'), may hold values from 0 to 4095
Outputs:
- slot_loss: float32 [512], P('dev')
- grad_hidden: float32 [1024, 512], replicated
- grad_out: float32 [512, 128], replicated
- item_grad: float32 [65536, 128], P('dev')
Inputs may be any that keep to these rules, and one draw needn't show every extreme that they name: `routes`: each row names 4 different clusters; within the rows of one device no cluster is named more than 8 times; every cluster is named by some row. `cluster_slot`: each cluster has one slot.
All inputs are finite; a program needn't handle non-finite values.
Results may differ from a plain program's by a relative error of at most 0.012.
The roundings to bfloat16 on the way count: a program that leaves them out, or rounds other values in their place, can miss the bound.
Values may be sent and summed in bfloat16 or wider, within the bound.
A program may use at most 128 MiB of HBM per device.

v0:
```python
import math

import jax
import jax.numpy as jnp
from jax import lax
from jax.sharding import PartitionSpec as P


def silu_grad(value):
    sig = jax.nn.sigmoid(value)
    return sig * (1.0 + value * (1.0 - sig))


def slot_ranks(keys):
    order = jnp.argsort(keys, stable=True)
    sorted_keys = keys[order]
    first = jnp.searchsorted(sorted_keys, sorted_keys, side="left")
    ranked = jnp.arange(keys.shape[0], dtype=jnp.int32) - first
    return jnp.zeros_like(keys).at[order].set(ranked)


def score_block(queries, targets, block_items, table_ids, counts):
    item_rows = block_items.shape[1]
    picks = (
        table_ids[:, :, None] == lax.broadcasted_iota(jnp.int32, table_ids.shape + (item_rows,), 2)
    ).astype(jnp.bfloat16)
    table = jnp.einsum(
        "csi,cie->cse", picks, block_items, preferred_element_type=jnp.float32
    ).astype(jnp.bfloat16)
    scores = jnp.einsum("cqe,cse->cqs", queries, table, preferred_element_type=jnp.float32)
    scores = scores - jnp.log(counts.astype(jnp.float32))[:, None, :]
    top = jnp.max(scores, axis=2, keepdims=True)
    expo = jnp.exp(scores - top)
    total = jnp.sum(expo, axis=2, keepdims=True)
    hit = lax.broadcasted_iota(jnp.int32, scores.shape, 2) == targets[:, :, None]
    picked = jnp.sum(jnp.where(hit, scores, 0.0), axis=2)
    losses = jnp.log(total[:, :, 0]) + top[:, :, 0] - picked
    live = targets >= 0
    cluster_loss = jnp.sum(jnp.where(live, losses, 0.0), axis=1) / jnp.sum(
        live.astype(jnp.float32), axis=1
    )
    weight = (expo / total - hit.astype(jnp.float32)).astype(jnp.bfloat16)
    wsum = jnp.einsum("cqs,csi->cqi", weight, picks, preferred_element_type=jnp.float32)
    dquery = jnp.einsum(
        "cqi,cie->cqe", wsum, block_items.astype(jnp.float32), precision=lax.Precision.HIGHEST
    ).astype(jnp.bfloat16)
    dtable = jnp.einsum(
        "cqi,cqe->cie", wsum, queries.astype(jnp.float32), precision=lax.Precision.HIGHEST
    )
    return (cluster_loss, dquery, dtable)


def owner_range(got_query, got_target, items, sample_ids, sample_counts, first, count):
    local_clusters = sample_ids.shape[0]
    width = items.shape[1]
    item_rows = items.shape[0] // local_clusters
    cluster_items = items.reshape(local_clusters, item_rows, width)
    block = math.gcd(count, 4)

    def step(carry, index):
        start = first + index * block
        queries = lax.dynamic_slice_in_dim(got_query, start, block, 0)
        targets = lax.dynamic_slice_in_dim(got_target, start, block, 0)
        table_ids = lax.dynamic_slice_in_dim(sample_ids, start, block, 0)
        counts = lax.dynamic_slice_in_dim(sample_counts, start, block, 0)
        block_items = lax.dynamic_slice_in_dim(cluster_items, start, block, 0)
        cluster_loss, dquery, dtable = score_block(queries, targets, block_items, table_ids, counts)
        return (carry, (cluster_loss, dquery, dtable))

    _, (losses, dquery, dtable) = lax.scan(
        step, jnp.zeros((), jnp.float32), jnp.arange(count // block, dtype=jnp.int32)
    )
    losses = losses.reshape((count,))
    dquery = dquery.reshape((count,) + dquery.shape[2:])
    grads = dtable.reshape((count * item_rows, width))
    return (grads, losses, dquery)


def local(
    features, w_hidden, w_out, items, routes, cluster_slot, sample_ids, sample_counts, positives
):
    devices = lax.axis_size("dev")
    users, visits = routes.shape
    clusters = cluster_slot.shape[0]
    local_clusters = sample_ids.shape[0]
    width = w_out.shape[1]
    capacity = max(2, 2 * users * visits // (local_clusters * devices))
    pre = jnp.dot(features, w_hidden, preferred_element_type=jnp.float32)
    hidden = jax.nn.silu(pre).astype(jnp.bfloat16)
    query = jnp.dot(hidden, w_out, preferred_element_type=jnp.float32).astype(jnp.bfloat16)
    flat_slots = jnp.take(cluster_slot, routes.reshape(-1), axis=0)
    ranks = slot_ranks(flat_slots)
    place = flat_slots * capacity + ranks
    send_query = (
        jnp.zeros((clusters * capacity, width), jnp.bfloat16)
        .at[place]
        .set(jnp.repeat(query, visits, axis=0))
    )
    send_target = (
        jnp.full((clusters * capacity,), -1, jnp.int32).at[place].set(positives.reshape(-1))
    )
    got_query, got_target = (
        lax.all_to_all(
            send_query.reshape(clusters, capacity, width),
            "dev",
            split_axis=0,
            concat_axis=1,
            tiled=True,
        ),
        lax.all_to_all(
            send_target.reshape(clusters, capacity), "dev", split_axis=0, concat_axis=1, tiled=True
        ),
    )
    grads, slot_loss, dq_all = owner_range(
        got_query, got_target, items, sample_ids, sample_counts, 0, local_clusters
    )
    returned = lax.all_to_all(dq_all, "dev", split_axis=1, concat_axis=0, tiled=True).reshape(
        clusters * capacity, width
    )
    dq_pairs = jnp.take(returned, place, axis=0).astype(jnp.float32).reshape(users, visits, width)
    dq_total = jnp.sum(dq_pairs, axis=1).astype(jnp.bfloat16)
    local_out = jnp.dot(hidden.T, dq_total, preferred_element_type=jnp.float32)
    dhidden = jnp.dot(dq_total, w_out.T, preferred_element_type=jnp.float32)
    dpre = (dhidden * silu_grad(pre)).astype(jnp.bfloat16)
    local_hidden = jnp.dot(features.T, dpre, preferred_element_type=jnp.float32)
    grad_hidden, grad_out = lax.psum((local_hidden, local_out), "dev")
    return (slot_loss, grad_hidden, grad_out, grads)


def solution(mesh):
    in_specs = (
        P("dev", None),
        P(),
        P(),
        P("dev", None),
        P("dev", None),
        P(),
        P("dev", None),
        P("dev", None),
        P("dev", None),
    )
    out_specs = (P("dev"), P(), P(), P("dev", None))
    return jax.shard_map(local, mesh=mesh, in_specs=in_specs, out_specs=out_specs, check_vma=False)
```

profile of v0, /device:TPU:0, one launch (start us, length us, event | category | flops | bytes accessed | tf_op | source)
XLA Modules:
  0.0 575.2 jit_solution(10307713451759058407)
XLA Ops:
  7.2 0.9 copy.33
  8.5 11.1 %gather_fusion.1 = s32[2048]{0:T(1024)S(1)} fusion(s32[512]{0:T(512)} %param.18, s32[2048]{0:T(1024)S(1)} %broadcast_clamp_fusion.3), kind=kCustom, calls=%fused_computation.1 | custom fusion | bytes 24576 | tf_op jit(solution)/shard_map/jit(_take)/gather | solution.py:91
  19.7 5.0 sort.17
  24.7 11.8 %gather_fusion.2 = s32[2048]{0:T(1024)S(1)} fusion(s32[2048]{0:T(1024)S(1)} %and_select_fusion, s32[2048]{0:T(1024)S(1)} %get-tuple-element.234), kind=kCustom, calls=%fused_computation.2 | custom fusion | bytes 24576 | tf_op jit(solution)/shard_map/gather | solution.py:16
  36.5 142.4 %while.40 = (s32[]{:T(128)}, u32[2048]{0:T(1024)S(1)}, u32[2048]{0:T(1024)S(1)}, s32[2048]{0:T(1024)S(1)}, s32[]{:T(128)}, /*index=5*/s32[]{:T(128)}, s32[]{}) while((s32[]{:T(128)}, u32[2048]{0:T(1024)S(1)}, u32[2048]{0:T(1024)S(1)}, s32[2048]{0:T(1024)S(1)}, s32[]{:T(128)}, /*index=5*/s32[]{:T(128)}, s32[]{}) %tuple.75), condition=%wide.region_2.3_spmd.clone, body=%wide.region_1.2_spmd.clone.sunk | while | flops 38916 | bytes 135277 | solution.py:17
  36.6 11.8 %gather_fusion = s32[2048]{0:T(1024)S(1)} fusion(s32[2048]{0:T(1024)S(1)} %get-tuple-element.361, u32[2048]{0:T(1024)S(1)} %broadcast_clamp_fusion.5), kind=kCustom, calls=%fused_computation.clone.clone.1 | custom fusion | bytes 24576 | tf_op jit(solution)/shard_map/jit(searchsorted)/jit(_searchsorted_scan_impl)/vmap(jit(_searchsorted_scan_impl))/while/body/eval_jaxpr/gather | solution.py:17
  48.4 11.8 %gather_fusion = s32[2048]{0:T(1024)S(1)} fusion(s32[2048]{0:T(1024)S(1)} %get-tuple-element.361, u32[2048]{0:T(1024)S(1)} %broadcast_clamp_fusion.5), kind=kCustom, calls=%fused_computation.clone.clone.1 | custom fusion | bytes 24576 | tf_op jit(solution)/shard_map/jit(searchsorted)/jit(_searchsorted_scan_impl)/vmap(jit(_searchsorted_scan_impl))/while/body/eval_jaxpr/gather | solution.py:17
  60.3 11.8 %gather_fusion = s32[2048]{0:T(1024)S(1)} fusion(s32[2048]{0:T(1024)S(1)} %get-tuple-element.361, u32[2048]{0:T(1024)S(1)} %broadcast_clamp_fusion.5), kind=kCustom, calls=%fused_computation.clone.clone.1 | custom fusion | bytes 24576 | tf_op jit(solution)/shard_map/jit(searchsorted)/jit(_searchsorted_scan_impl)/vmap(jit(_searchsorted_scan_impl))/while/body/eval_jaxpr/gather | solution.py:17
  72.2 11.8 %gather_fusion = s32[2048]{0:T(1024)S(1)} fusion(s32[2048]{0:T(1024)S(1)} %get-tuple-element.361, u32[2048]{0:T(1024)S(1)} %broadcast_clamp_fusion.5), kind=kCustom, calls=%fused_computation.clone.clone.1 | custom fusion | bytes 24576 | tf_op jit(solution)/shard_map/jit(searchsorted)/jit(_searchsorted_scan_impl)/vmap(jit(_searchsorted_scan_impl))/while/body/eval_jaxpr/gather | solution.py:17
  84.0 11.8 %gather_fusion = s32[2048]{0:T(1024)S(1)} fusion(s32[2048]{0:T(1024)S(1)} %get-tuple-element.361, u32[2048]{0:T(1024)S(1)} %broadcast_clamp_fusion.5), kind=kCustom, calls=%fused_computation.clone.clone.1 | custom fusion | bytes 24576 | tf_op jit(solution)/shard_map/jit(searchsorted)/jit(_searchsorted_scan_impl)/vmap(jit(_searchsorted_scan_impl))/while/body/eval_jaxpr/gather | solution.py:17
  95.9 11.8 %gather_fusion = s32[2048]{0:T(1024)S(1)} fusion(s32[2048]{0:T(1024)S(1)} %get-tuple-element.361, u32[2048]{0:T(1024)S(1)} %broadcast_clamp_fusion.5), kind=kCustom, calls=%fused_computation.clone.clone.1 | custom fusion | bytes 24576 | tf_op jit(solution)/shard_map/jit(searchsorted)/jit(_searchsorted_scan_impl)/vmap(jit(_searchsorted_scan_impl))/while/body/eval_jaxpr/gather | solution.py:17
  107.8 11.8 %gather_fusion = s32[2048]{0:T(1024)S(1)} fusion(s32[2048]{0:T(1024)S(1)} %get-tuple-element.361, u32[2048]{0:T(1024)S(1)} %broadcast_clamp_fusion.5), kind=kCustom, calls=%fused_computation.clone.clone.1 | custom fusion | bytes 24576 | tf_op jit(solution)/shard_map/jit(searchsorted)/jit(_searchsorted_scan_impl)/vmap(jit(_searchsorted_scan_impl))/while/body/eval_jaxpr/gather | solution.py:17
  119.6 11.8 %gather_fusion = s32[2048]{0:T(1024)S(1)} fusion(s32[2048]{0:T(1024)S(1)} %get-tuple-element.361, u32[2048]{0:T(1024)S(1)} %broadcast_clamp_fusion.5), kind=kCustom, calls=%fused_computation.clone.clone.1 | custom fusion | bytes 24576 | tf_op jit(solution)/shard_map/jit(searchsorted)/jit(_searchsorted_scan_impl)/vmap(jit(_searchsorted_scan_impl))/while/body/eval_jaxpr/gather | solution.py:17
  131.5 11.8 %gather_fusion = s32[2048]{0:T(1024)S(1)} fusion(s32[2048]{0:T(1024)S(1)} %get-tuple-element.361, u32[2048]{0:T(1024)S(1)} %broadcast_clamp_fusion.5), kind=kCustom, calls=%fused_computation.clone.clone.1 | custom fusion | bytes 24576 | tf_op jit(solution)/shard_map/jit(searchsorted)/jit(_searchsorted_scan_impl)/vmap(jit(_searchsorted_scan_impl))/while/body/eval_jaxpr/gather | solution.py:17
  143.4 11.8 %gather_fusion = s32[2048]{0:T(1024)S(1)} fusion(s32[2048]{0:T(1024)S(1)} %get-tuple-element.361, u32[2048]{0:T(1024)S(1)} %broadcast_clamp_fusion.5), kind=kCustom, calls=%fused_computation.clone.clone.1 | custom fusion | bytes 24576 | tf_op jit(solution)/shard_map/jit(searchsorted)/jit(_searchsorted_scan_impl)/vmap(jit(_searchsorted_scan_impl))/while/body/eval_jaxpr/gather | solution.py:17
  155.2 11.8 %gather_fusion = s32[2048]{0:T(1024)S(1)} fusion(s32[2048]{0:T(1024)S(1)} %get-tuple-element.361, u32[2048]{0:T(1024)S(1)} %broadcast_clamp_fusion.5), kind=kCustom, calls=%fused_computation.clone.clone.1 | custom fusion | bytes 24576 | tf_op jit(solution)/shard_map/jit(searchsorted)/jit(_searchsorted_scan_impl)/vmap(jit(_searchsorted_scan_impl))/while/body/eval_jaxpr/gather | solution.py:17
  167.1 11.8 %gather_fusion = s32[2048]{0:T(1024)S(1)} fusion(s32[2048]{0:T(1024)S(1)} %get-tuple-element.361, u32[2048]{0:T(1024)S(1)} %broadcast_clamp_fusion.5), kind=kCustom, calls=%fused_computation.clone.clone.1 | custom fusion | bytes 24576 | tf_op jit(solution)/shard_map/jit(searchsorted)/jit(_searchsorted_scan_impl)/vmap(jit(_searchsorted_scan_impl))/while/body/eval_jaxpr/gather | solution.py:17
  179.0 8.0 %scatter_custom_fusion = s32[2048]{0:T(1024)S(1)} fusion(s32[2048]{0:T(1024)S(1)} %get-tuple-element.235, s32[2048]{0:T(1024)S(1)} %convert_subtract_fusion, s32[]{:T(128)} %constant.92.clone.1), kind=kCustom, calls=%fused_computation.70 | custom fusion | bytes 8196 | tf_op jit(solution)/shard_map/scatter | solution.py:19
  187.9 8.1 %scatter_custom_fusion.1 = s32[4096]{0:T(1024)S(1)} fusion(s32[2048]{0:T(1024)S(1)} %get-tuple-element.231, s32[2048]{0:T(1024)S(1)} %reshape.162, s32[]{:T(128)} %constant.104.clone.1), kind=kCustom, calls=%fused_computation.63 | custom fusion | bytes 16388 | tf_op jit(solution)/shard_map/scatter | solution.py:100
  197.0 7.3 %all-to-all-start = ((s32[32,1,128]{2,1,0:T(1,128)}), s32[32,1,128]{2,1,0:T(1,128)S(1)}, u32[]{:S(2)}, u32[]{:S(2)}) async-start(s32[32,1,128]{2,1,0:T(1,128)} %reshape.189), calls=%async_computation | async-start | bytes 32768 | tf_op jit(solution)/shard_map/all_to_all | solution.py:110
  204.4 1.8 multiply_convert_fusion
  207.4 6.8 %scatter_custom_fusion.2 = bf16[4096,128]{1,0:T(8,128)(2,1)} fusion(s32[2048]{0:T(1024)S(1)} %get-tuple-element.231, bf16[2048,128]{1,0:T(8,128)(2,1)S(1)} %bitcast.65, bf16[]{:T(256)} %constant.94.clone.1), kind=kCustom, calls=%fused_computation.56 | custom fusion | bytes 1048578 | tf_op jit(solution)/shard_map/scatter | solution.py:97
  214.2 6.0 %all-to-all-start.1 = ((bf16[512,8,128]{2,1,0:T(8,128)(2,1)}), bf16[512,8,128]{2,1,0:T(8,128)(2,1)S(1)}, u32[]{:S(2)}, u32[]{:S(2)}) async-start(bf16[512,8,128]{2,1,0:T(8,128)(2,1)} %bitcast.8), calls=%async_computation.1 | async-start | bytes 2097152 | tf_op jit(solution)/shard_map/all_to_all | solution.py:103
  221.7 24.6 %all-to-all-done.1 = bf16[512,8,128]{2,1,0:T(8,128)(2,1)S(1)} async-done(((bf16[512,8,128]{2,1,0:T(8,128)(2,1)}), bf16[512,8,128]{2,1,0:T(8,128)(2,1)S(1)}, u32[]{:S(2)}, u32[]{:S(2)}) %all-to-all-start.1) | async-done | bytes 1048608 | tf_op jit(solution)/shard_map/all_to_all | solution.py:103
  246.6 137.4 %while.39 = (s32[]{:T(128)}, f32[4,4]{1,0:T(4,128)S(1)}, bf16[4,4,256,128]{3,1,0,2:T(4,128)(2,1)}, f32[4,4,128,128]{3,2,1,0:T(8,128)}, s32[4]{0:T(128)S(1)}, /*i...) while((s32[]{:T(128)}, f32[4,4]{1,0:T(4,128)S(1)}, ...), condition=%wide.region_12.13_spmd, body=%wide.region_6.12_spmd.sunk | while | flops 3156365312 | bytes 54386004 | solution.py:70
  247.9 0.9 convert_log_fusion.2
  248.8 0.9 constant_dynamic-slice_fusion.4
  249.7 8.3 %subtract_reduce_fusion.2 = (f32[4,256]{1,0:T(4,128)S(1)}, f32[4,256,4096]{2,1,0:T(8,128)}) fusion(f32[4,4096]{1,0:T(4,128)S(1)} %convert_log_fusion.2, s32[4,4096]{1,0:T(4,128)S(1)} %constant_dynamic-slice_fusion.4, bf16[16,128,128]{2,1,0:T(8,128)(2,1)} %get-tuple-element.401, s32[]{:T(128)S(6)} %select_n.90, ...), kind=kOutput, calls=%fused_computation.12.clone.1 | convolution fusion | flops 1623194624 | bytes 17306624 | tf_op jit(solution)/shard_map/while/body/eval_jaxpr/cqe,cse->cqs/dot_general | solution.py:30
  258.0 8.8 %fusion.59 = (f32[4,256]{1,0:T(4,128)S(1)}, f32[4,256]{1,0:T(4,128)S(1)}) fusion(f32[4,256,4096]{2,1,0:T(8,128)} %get-tuple-element.331, f32[4,256]{1,0:T(4,128)S(1)} %get-tuple-element.332, f32[4,4096]{1,0:T(4,128)S(1)} %convert_log_fusion.2, s32[4,256]{1,0:T(4,128)S(1)} %get-tuple-element.333), kind=kLoop, calls=%fused_computation.11.clone.1 | loop fusion | flops 25163776 | bytes 16859136 | tf_op jit(solution)/shard_map/while/body/eval_jaxpr/reduce_sum | solution.py:34
  267.0 10.3 %fusion.60 = f32[4,256,128]{2,1,0:T(8,128)S(1)} fusion(f32[4,256,4096]{2,1,0:T(8,128)} %get-tuple-element.331, f32[4,256]{1,0:T(4,128)S(1)} %get-tuple-element.335, s32[4,256]{1,0:T(4,128)S(1)} %get-tuple-element.333, f32[4,256]{1,0:T(4,128)S(1)} %get-tuple-element.332, f32[4,4096]{1,0:T(4,128)S(1)} %convert_log_fusion.2, ...), kind=kOutput, calls=%fused_computation.14.clone.1 | convolution fusion | flops 1105199104 | bytes 17444864 | tf_op jit(solution)/shard_map/while/body/eval_jaxpr/cqs,csi->cqi/dot_general | solution.py:43
  277.4 1.3 fusion.61
  278.7 0.9 copy_dynamic-update-slice_fusion.2
  279.6 1.4 fusion.62
  282.2 0.9 convert_log_fusion.2
  283.2 0.9 constant_dynamic-slice_fusion.4
  284.1 8.3 %subtract_reduce_fusion.2 = (f32[4,256]{1,0:T(4,128)S(1)}, f32[4,256,4096]{2,1,0:T(8,128)}) fusion(f32[4,4096]{1,0:T(4,128)S(1)} %convert_log_fusion.2, s32[4,4096]{1,0:T(4,128)S(1)} %constant_dynamic-slice_fusion.4, bf16[16,128,128]{2,1,0:T(8,128)(2,1)} %get-tuple-element.401, s32[]{:T(128)S(6)} %select_n.90, ...), kind=kOutput, calls=%fused_computation.12.clone.1 | convolution fusion | flops 1623194624 | bytes 17306624 | tf_op jit(solution)/shard_map/while/body/eval_jaxpr/cqe,cse->cqs/dot_general | solution.py:30
  292.4 8.8 %fusion.59 = (f32[4,256]{1,0:T(4,128)S(1)}, f32[4,256]{1,0:T(4,128)S(1)}) fusion(f32[4,256,4096]{2,1,0:T(8,128)} %get-tuple-element.331, f32[4,256]{1,0:T(4,128)S(1)} %get-tuple-element.332, f32[4,4096]{1,0:T(4,128)S(1)} %convert_log_fusion.2, s32[4,256]{1,0:T(4,128)S(1)} %get-tuple-element.333), kind=kLoop, calls=%fused_computation.11.clone.1 | loop fusion | flops 25163776 | bytes 16859136 | tf_op jit(solution)/shard_map/while/body/eval_jaxpr/reduce_sum | solution.py:34
  301.4 10.3 %fusion.60 = f32[4,256,128]{2,1,0:T(8,128)S(1)} fusion(f32[4,256,4096]{2,1,0:T(8,128)} %get-tuple-element.331, f32[4,256]{1,0:T(4,128)S(1)} %get-tuple-element.335, s32[4,256]{1,0:T(4,128)S(1)} %get-tuple-element.333, f32[4,256]{1,0:T(4,128)S(1)} %get-tuple-element.332, f32[4,4096]{1,0:T(4,128)S(1)} %convert_log_fusion.2, ...), kind=kOutput, calls=%fused_computation.14.clone.1 | convolution fusion | flops 1105199104 | bytes 17444864 | tf_op jit(solution)/shard_map/while/body/eval_jaxpr/cqs,csi->cqi/dot_general | solution.py:43
  311.7 1.3 fusion.61
  313.0 0.9 copy_dynamic-update-slice_fusion.2
  313.9 1.4 fusion.62
  316.6 0.9 convert_log_fusion.2
  317.5 0.9 constant_dynamic-slice_fusion.4
  318.4 8.3 %subtract_reduce_fusion.2 = (f32[4,256]{1,0:T(4,128)S(1)}, f32[4,256,4096]{2,1,0:T(8,128)}) fusion(f32[4,4096]{1,0:T(4,128)S(1)} %convert_log_fusion.2, s32[4,4096]{1,0:T(4,128)S(1)} %constant_dynamic-slice_fusion.4, bf16[16,128,128]{2,1,0:T(8,128)(2,1)} %get-tuple-element.401, s32[]{:T(128)S(6)} %select_n.90, ...), kind=kOutput, calls=%fused_computation.12.clone.1 | convolution fusion | flops 1623194624 | bytes 17306624 | tf_op jit(solution)/shard_map/while/body/eval_jaxpr/cqe,cse->cqs/dot_general | solution.py:30
  326.7 8.8 %fusion.59 = (f32[4,256]{1,0:T(4,128)S(1)}, f32[4,256]{1,0:T(4,128)S(1)}) fusion(f32[4,256,4096]{2,1,0:T(8,128)} %get-tuple-element.331, f32[4,256]{1,0:T(4,128)S(1)} %get-tuple-element.332, f32[4,4096]{1,0:T(4,128)S(1)} %convert_log_fusion.2, s32[4,256]{1,0:T(4,128)S(1)} %get-tuple-element.333), kind=kLoop, calls=%fused_computation.11.clone.1 | loop fusion | flops 25163776 | bytes 16859136 | tf_op jit(solution)/shard_map/while/body/eval_jaxpr/reduce_sum | solution.py:34
  335.8 10.3 %fusion.60 = f32[4,256,128]{2,1,0:T(8,128)S(1)} fusion(f32[4,256,4096]{2,1,0:T(8,128)} %get-tuple-element.331, f32[4,256]{1,0:T(4,128)S(1)} %get-tuple-element.335, s32[4,256]{1,0:T(4,128)S(1)} %get-tuple-element.333, f32[4,256]{1,0:T(4,128)S(1)} %get-tuple-element.332, f32[4,4096]{1,0:T(4,128)S(1)} %convert_log_fusion.2, ...), kind=kOutput, calls=%fused_computation.14.clone.1 | convolution fusion | flops 1105199104 | bytes 17444864 | tf_op jit(solution)/shard_map/while/body/eval_jaxpr/cqs,csi->cqi/dot_general | solution.py:43
  346.1 1.3 fusion.61
  348.3 1.4 fusion.62
  350.9 0.9 convert_log_fusion.2
  351.9 0.9 constant_dynamic-slice_fusion.4
  352.8 8.3 %subtract_reduce_fusion.2 = (f32[4,256]{1,0:T(4,128)S(1)}, f32[4,256,4096]{2,1,0:T(8,128)}) fusion(f32[4,4096]{1,0:T(4,128)S(1)} %convert_log_fusion.2, s32[4,4096]{1,0:T(4,128)S(1)} %constant_dynamic-slice_fusion.4, bf16[16,128,128]{2,1,0:T(8,128)(2,1)} %get-tuple-element.401, s32[]{:T(128)S(6)} %select_n.90, ...), kind=kOutput, calls=%fused_computation.12.clone.1 | convolution fusion | flops 1623194624 | bytes 17306624 | tf_op jit(solution)/shard_map/while/body/eval_jaxpr/cqe,cse->cqs/dot_general | solution.py:30
  361.1 8.8 %fusion.59 = (f32[4,256]{1,0:T(4,128)S(1)}, f32[4,256]{1,0:T(4,128)S(1)}) fusion(f32[4,256,4096]{2,1,0:T(8,128)} %get-tuple-element.331, f32[4,256]{1,0:T(4,128)S(1)} %get-tuple-element.332, f32[4,4096]{1,0:T(4,128)S(1)} %convert_log_fusion.2, s32[4,256]{1,0:T(4,128)S(1)} %get-tuple-element.333), kind=kLoop, calls=%fused_computation.11.clone.1 | loop fusion | flops 25163776 | bytes 16859136 | tf_op jit(solution)/shard_map/while/body/eval_jaxpr/reduce_sum | solution.py:34
  370.1 10.3 %fusion.60 = f32[4,256,128]{2,1,0:T(8,128)S(1)} fusion(f32[4,256,4096]{2,1,0:T(8,128)} %get-tuple-element.331, f32[4,256]{1,0:T(4,128)S(1)} %get-tuple-element.335, s32[4,256]{1,0:T(4,128)S(1)} %get-tuple-element.333, f32[4,256]{1,0:T(4,128)S(1)} %get-tuple-element.332, f32[4,4096]{1,0:T(4,128)S(1)} %convert_log_fusion.2, ...), kind=kOutput, calls=%fused_computation.14.clone.1 | convolution fusion | flops 1105199104 | bytes 17444864 | tf_op jit(solution)/shard_map/while/body/eval_jaxpr/cqs,csi->cqi/dot_general | solution.py:43
  380.4 1.3 fusion.61
  382.6 1.4 fusion.62
  384.0 3.6 all-to-all-start.2
  388.0 25.8 %all-to-all-done.2 = bf16[16,256,128]{2,0,1:T(8,128)(2,1)S(1)} async-done(((bf16[16,256,128]{2,0,1:T(8,128)(2,1)}), bf16[16,256,128]{2,0,1:T(8,128)(2,1)S(1)}, u32[]{:S(2)}, u32[]{:S(2)}) %all-to-all-start.2) | async-done | bytes 1048608 | tf_op jit(solution)/shard_map/all_to_all | solution.py:117
  414.1 6.2 %gather_fusion.3 = bf16[2048,128]{1,0:T(8,128)(2,1)S(1)} fusion(bf16[4096,128]{1,0:T(8,128)(2,1)S(1)} %bitcast.58, s32[2048]{0:T(1024)S(1)} %broadcast_clamp_fusion.1), kind=kCustom, calls=%fused_computation.3 | custom fusion | bytes 1056768 | tf_op jit(solution)/shard_map/jit(_take)/gather | solution.py:120
  420.3 2.9 select_reduce_fusion.2
  423.3 2.1 fusion.33
  425.3 3.6 convolution_bitcast_fusion.1
  429.5 134.3 %all-reduce.3.cloned.1.call-done = (f32[1024,512]{0,1:T(8,128)}, f32[512,128]{1,0:T(8,128)}) async-done(((f32[1024,512]{0,1:T(8,128)}, f32[512,128]{1,0:T(8,128)}), (f32[1024,512]{0,1:T(8,128)}, f32[512,128]{1,0:T(8,128)})) %all-reduce.3.cloned.1.call-update) | async-done | bytes 2359312 | tf_op jit(solution)/shard_map/psum | solution.py:126
  563.8 2.9 copy.42
  566.7 1.7 copy.79
  (123 shorter events, 11.8 us)
Async XLA Ops:
  7.2 197.2 %copy-start = (bf16[512,1024]{1,0:T(8,128)(2,1)S(1)}, bf16[512,1024]{1,0:T(8,128)(2,1)}, u32[]{:S(2)}) copy-start(bf16[512,1024]{1,0:T(8,128)(2,1)} %param.13) | copy-start | bytes 3145732
  36.5 151.1 %copy-start.6 = (s32[512,4]{0,1:T(4,128)S(1)}, s32[512,4]{0,1:T(4,128)}, u32[]{:S(2)}) copy-start(s32[512,4]{0,1:T(4,128)} %param.21) | copy-start | bytes 24580
  36.5 167.8 %copy-start.8 = (bf16[1024,512]{1,0:T(8,128)(2,1)S(1)}, bf16[1024,512]{1,0:T(8,128)(2,1)}, u32[]{:S(2)}) copy-start(bf16[1024,512]{1,0:T(8,128)(2,1)} %param.14) | copy-start | bytes 3145732
  36.5 170.4 %copy-start.2 = (bf16[512,128]{1,0:T(8,128)(2,1)S(1)}, bf16[512,128]{1,0:T(8,128)(2,1)}, u32[]{:S(2)}) copy-start(bf16[512,128]{1,0:T(8,128)(2,1)} %param.15) | copy-start | bytes 393220
  187.6 58.7 %copy-start.4 = (s32[2048]{0:T(1024)}, s32[2048]{0:T(1024)S(1)}, u32[]{:S(2)}) copy-start(s32[2048]{0:T(1024)S(1)} %get-tuple-element.231) | copy-start | bytes 24580
  197.0 17.2 %all-to-all-start = ((s32[32,1,128]{2,1,0:T(1,128)}), s32[32,1,128]{2,1,0:T(1,128)S(1)}, u32[]{:S(2)}, u32[]{:S(2)}) async-start(s32[32,1,128]{2,1,0:T(1,128)} %reshape.189), calls=%async_computation | async-start | bytes 32768 | tf_op jit(solution)/shard_map/all_to_all | solution.py:110
  206.1 0.8 copy-start.1
  214.2 32.0 %all-to-all-start.1 = ((bf16[512,8,128]{2,1,0:T(8,128)(2,1)}), bf16[512,8,128]{2,1,0:T(8,128)(2,1)S(1)}, u32[]{:S(2)}, u32[]{:S(2)}) async-start(bf16[512,8,128]{2,1,0:T(8,128)(2,1)} %bitcast.8), calls=%async_computation.1 | async-start | bytes 2097152 | tf_op jit(solution)/shard_map/all_to_all | solution.py:103
  246.6 141.1 %copy-start.7 = (pred[2048]{0:T(1024)(128)(4,1)S(1)}, pred[2048]{0:T(1024)(128)(4,1)}, u32[]{:S(2)}) copy-start(pred[2048]{0:T(1024)(128)(4,1)} %get-tuple-element.230) | copy-start | bytes 6148
  246.6 141.4 %copy-start.5 = (s32[2048]{0:T(1024)S(1)}, s32[2048]{0:T(1024)}, u32[]{:S(2)}) copy-start(s32[2048]{0:T(1024)} %copy-done.4) | copy-start | bytes 24580
  246.6 178.8 %copy-start.3 = (bf16[512,128]{1,0:T(8,128)(2,1)S(1)}, bf16[512,128]{1,0:T(8,128)(2,1)}, u32[]{:S(2)}) copy-start(bf16[512,128]{1,0:T(8,128)(2,1)} %param.15) | copy-start | bytes 393220
  384.0 29.8 %all-to-all-start.2 = ((bf16[16,256,128]{2,0,1:T(8,128)(2,1)}), bf16[16,256,128]{2,0,1:T(8,128)(2,1)S(1)}, u32[]{:S(2)}, u32[]{:S(2)}) async-start(bf16[16,256,128]{2,0,1:T(8,128)(2,1)} %bitcast.64), calls=%async_computation.2 | async-start | bytes 2097152 | tf_op jit(solution)/shard_map/all_to_all | solution.py:117
  387.6 176.2 %all-reduce.3.cloned.1.call-start = ((), (), s32[]{:S(2)}) async-start(), calls=%async_computation.3 | async-start | bytes 4718592 | tf_op jit(solution)/shard_map/psum | solution.py:126
Sparse Core Ops, SparseCore 0:
  429.0 134.7 all-reduce.2
where the time goes:
time: 577 us; the launch traced here: 575 us
  local copies, waits for them, and re-layouts  214 us (37%)
  waiting for transfers between devices  185 us (32%)
  matrix products  92.8 us (16%)
  other arithmetic  49.3 us (9%)
  starting transfers between devices  17 us (3%)
  between operations  14.4 us (2%)
    gather x12, local copies, waits for them, and re-layouts, slot_ranks(): first = jnp.searchsorted(sorted_keys, sorted_keys, side='left')  141 us
    psum x1, waiting for transfers between devices, local(): grad_hidden, grad_out = lax.psum((local_hidden, local_out), 'dev')  134 us
    dot_general x4, matrix products, score_block(): jnp.einsum('cqs,csi->cqi', weight, picks, preferred_element_type=jnp.floa...  41.3 us
    reduce_sum x4, other arithmetic, score_block(): total = jnp.sum(expo, axis=2, keepdims=True)  35.3 us
    dot_general x4, matrix products, score_block(): jnp.einsum('cqe,cse->cqs', queries, table, preferred_element_type=jnp.flo...  33.2 us
    all_to_all x1, waiting for transfers between devices, local(): lax.all_to_all(dq_all, 'dev', split_axis=1, concat_axis=0, tiled=True)  25.8 us
    all_to_all x1, waiting for transfers between devices, local(): lax.all_to_all(send_query.reshape(clusters, capacity, width), 'dev', spli...  24.6 us
    gather x1, local copies, waits for them, and re-layouts, slot_ranks(): sorted_keys = keys[order]  11.8 us
  transfers between devices with their start and end apart: 4, of which 3 were waited for; matrix products, arithmetic and copies ran while one was open for 2% of the time, Pallas kernels for 0%

commit v1 on v0

v1 whole, which is shorter than its diff:
```python
import jax
import jax.numpy as jnp
from jax import lax
from jax.sharding import PartitionSpec as P


def silu_grad(value):
    sig = jax.nn.sigmoid(value)
    return sig * (1.0 + value * (1.0 - sig))


def slot_codes(routes_t, positives_t, cluster_slot, capacity):
    visits, users = routes_t.shape
    clusters = cluster_slot.shape[0]
    ids = lax.broadcasted_iota(jnp.int32, (visits, clusters, users), 1)
    slots = jnp.sum(
        jnp.where(routes_t[:, None, :] == ids, cluster_slot[None, :, None], 0), axis=1
    )
    rows = lax.broadcasted_iota(jnp.int32, (clusters, users), 0)
    member = jnp.zeros((clusters, users), jnp.bool_)
    target = jnp.zeros((clusters, users), jnp.int32)
    for r in range(visits):
        same = slots[r][None, :] == rows
        member = member | same
        target = jnp.where(same, positives_t[r][None, :] + 1, target)
    earlier = lax.broadcasted_iota(jnp.int32, (users, users), 0) < lax.broadcasted_iota(
        jnp.int32, (users, users), 1
    )
    rank = jnp.dot(
        member.astype(jnp.bfloat16),
        earlier.astype(jnp.bfloat16),
        preferred_element_type=jnp.float32,
    )
    code = jnp.where(member, rank, -1.0).astype(jnp.bfloat16)
    return code, target


def owner(queries, targets, block_items, table_ids, counts):
    clusters, samples = table_ids.shape
    item_rows = block_items.shape[1]
    recip = 1.0 / counts.astype(jnp.float32)
    which = lax.broadcasted_iota(jnp.int32, (clusters, item_rows, samples), 1)
    mass = jnp.sum(jnp.where(table_ids[:, None, :] == which, recip[:, None, :], 0.0), axis=2)
    log_mass = jnp.log(mass)
    lanes = 128
    groups = samples // lanes
    low = targets % lanes
    high = targets // lanes
    pick_low = (
        low[:, :, None] == lax.broadcasted_iota(jnp.int32, low.shape + (lanes,), 2)
    ).astype(jnp.bfloat16)
    table = jnp.concatenate([table_ids, counts // 64, counts % 64], axis=1)
    table = table.reshape(clusters, 3 * groups, lanes).astype(jnp.bfloat16)
    near = jnp.einsum("cql,chl->cqh", pick_low, table, preferred_element_type=jnp.float32)
    column = lax.broadcasted_iota(jnp.int32, near.shape, 2)
    parts = [
        jnp.sum(jnp.where(column == high[:, :, None] + groups * t, near, 0.0), axis=2)
        for t in range(3)
    ]
    live = targets >= 0
    own_id = parts[0].astype(jnp.int32)
    own_count = jnp.where(live, parts[1] * 64.0 + parts[2], 1.0)
    scores = jnp.einsum("cqe,cie->cqi", queries, block_items, preferred_element_type=jnp.float32)
    shifted = scores + log_mass[:, None, :]
    top = jnp.max(shifted, axis=2, keepdims=True)
    expo = jnp.exp(shifted - top)
    total = jnp.sum(expo, axis=2, keepdims=True)
    hit = (
        lax.broadcasted_iota(jnp.int32, scores.shape, 2)
        == jnp.where(live, own_id, -1)[:, :, None]
    )
    picked = jnp.sum(jnp.where(hit, scores, 0.0), axis=2) - jnp.log(own_count)
    losses = jnp.log(total[:, :, 0]) + top[:, :, 0] - picked
    cluster_loss = jnp.sum(jnp.where(live, losses, 0.0), axis=1) / jnp.sum(
        live.astype(jnp.float32), axis=1
    )
    wsum = expo / total - hit.astype(jnp.float32)
    coarse = lax.reduce_precision(wsum, 8, 7)
    fine = (wsum - coarse).astype(jnp.bfloat16)
    coarse = coarse.astype(jnp.bfloat16)

    def both(equation, other):
        return jnp.einsum(
            equation, coarse, other, preferred_element_type=jnp.float32
        ) + jnp.einsum(equation, fine, other, preferred_element_type=jnp.float32)

    dquery = both("cqi,cie->cqe", block_items).astype(jnp.bfloat16)
    dtable = both("cqi,cqe->cie", queries)
    return cluster_loss, dquery, dtable


def local(
    features, w_hidden, w_out, items, routes, cluster_slot, sample_ids, sample_counts, positives
):
    devices = lax.axis_size("dev")
    users, visits = routes.shape
    clusters = cluster_slot.shape[0]
    local_clusters = sample_ids.shape[0]
    width = w_out.shape[1]
    item_rows = items.shape[0] // local_clusters
    capacity = max(2, 2 * users * visits // (local_clusters * devices))
    rows = local_clusters * capacity
    code, target = slot_codes(routes.T, positives.T, cluster_slot, capacity)
    seats = lax.broadcasted_iota(jnp.int32, (1, capacity, 1), 1).astype(jnp.bfloat16)
    seated = code[:, None, :] == seats
    select = seated.astype(jnp.bfloat16).reshape(clusters * capacity, users)
    send_target = jnp.sum(jnp.where(seated, target[:, None, :], 0), axis=2)
    send_target = send_target.reshape(devices, rows)
    coded = jnp.concatenate([send_target // 64, send_target % 64], axis=1)
    extra = -(-coded.shape[1] // (16 * width)) * 16
    coded = jnp.pad(coded, ((0, 0), (0, extra * width - coded.shape[1])))
    coded = coded.astype(jnp.bfloat16).reshape(devices, extra, width)
    pre = jnp.dot(features, w_hidden, preferred_element_type=jnp.float32)
    hidden = jax.nn.silu(pre).astype(jnp.bfloat16)
    query = jnp.dot(hidden, w_out, preferred_element_type=jnp.float32).astype(jnp.bfloat16)
    send_query = jnp.dot(select, query, preferred_element_type=jnp.float32).astype(jnp.bfloat16)
    payload = jnp.concatenate([send_query.reshape(devices, rows, width), coded], axis=1)
    got = lax.all_to_all(payload, "dev", split_axis=0, concat_axis=0, tiled=True)
    got_query = got[:, :rows].reshape(devices, local_clusters, capacity, width)
    got_query = got_query.transpose(1, 0, 2, 3).reshape(local_clusters, devices * capacity, width)
    got_coded = got[:, rows:].reshape(devices, extra * width).astype(jnp.int32)
    got_target = got_coded[:, :rows] * 64 + got_coded[:, rows : 2 * rows] - 1
    got_target = got_target.reshape(devices, local_clusters, capacity)
    got_target = got_target.transpose(1, 0, 2).reshape(local_clusters, devices * capacity)
    slot_loss, dquery, dtable = owner(
        got_query,
        got_target,
        items.reshape(local_clusters, item_rows, width),
        sample_ids,
        sample_counts,
    )
    back = dquery.reshape(local_clusters, devices, capacity, width).transpose(1, 0, 2, 3)
    returned = lax.all_to_all(
        back.reshape(devices, rows, width), "dev", split_axis=0, concat_axis=0, tiled=True
    ).reshape(clusters * capacity, width)
    dq_total = lax.dot_general(
        select, returned, (((0,), (0,)), ((), ())), preferred_element_type=jnp.float32
    ).astype(jnp.bfloat16)
    local_out = jnp.dot(hidden.T, dq_total, preferred_element_type=jnp.float32)
    dhidden = jnp.dot(dq_total, w_out.T, preferred_element_type=jnp.float32)
    dpre = (dhidden * silu_grad(pre)).astype(jnp.bfloat16)
    local_hidden = jnp.dot(features.T, dpre, preferred_element_type=jnp.float32)
    grad_hidden, grad_out = lax.psum((local_hidden, local_out), "dev")
    return (slot_loss, grad_hidden, grad_out, dtable.reshape(items.shape[0], width))


def solution(mesh):
    in_specs = (
        P("dev", None),
        P(),
        P(),
        P("dev", None),
        P("dev", None),
        P(),
        P("dev", None),
        P("dev", None),
        P("dev", None),
    )
    out_specs = (P("dev"), P(), P(), P("dev", None))
    return jax.shard_map(local, mesh=mesh, in_specs=in_specs, out_specs=out_specs, check_vma=False)
```

time: 577 us -> 256 us (0.44)
  local copies, waits for them, and re-layouts: 214 us -> 6.39 us
  matrix products: 92.8 us -> 24.4 us
  other arithmetic: 49.3 us -> 20.1 us
  waiting for transfers between devices: 185 us -> 178 us
    gather x15 -> x0, local copies, waits for them, and re-layouts: 170 us -> none  [the longest x12 141 us: slot_ranks(): first = jnp.searchsorted(sorted_keys, sorted_keys, side='left')]
    dot_general x17 -> x9, matrix products: 85.4 us -> 16.8 us  [the longest x1 3.91 us: local(): lax.dot_general(select, returned, (((0,), (0,)), ((), ())), preferred_ele...]
    scatter x3 -> x0, local copies, waits for them, and re-layouts: 22.9 us -> none  [the longest x1 8.06 us: local(): jnp.full((clusters * capacity,), -1, jnp.int32).at[place]]
    reduce_sum x9 -> x5, other arithmetic: 38.8 us -> 16.8 us  [the longest x1 8.96 us: local(): send_target = jnp.sum(jnp.where(seated, target[:, None, :], 0), axis=2)]
    dynamic_slice x8 -> x0, local copies, waits for them, and re-layouts: 6.03 us -> none  [the longest x4 3.7 us: step(): table_ids = lax.dynamic_slice_in_dim(sample_ids, start, block, 0)]
    all_to_all x3 -> x2, starting transfers between devices: 17 us -> 11.3 us  [the longest x1 7.5 us: local(): lax.all_to_all(payload, 'dev', split_axis=0, concat_axis=0, tiled=True)]
    all_to_all x3 -> x2, waiting for transfers between devices: 50.4 us -> 48.3 us  [the longest x1 25.2 us: local(): lax.all_to_all(back.reshape(devices, rows, width), 'dev', split_axis=0, c...]
  transfers between devices with their start and end apart: 4 -> 3, of which waited for: 3 -> 3; matrix products, arithmetic and copies ran while one was open for 2% -> 4% of each run, Pallas kernels for 0% -> 0%
where the time goes in v1:
time: 256 us; the launch traced here: 255 us
  waiting for transfers between devices  178 us (70%)
  matrix products  24.4 us (10%)
  other arithmetic  20.1 us (8%)
  between operations  14.5 us (6%)
  starting transfers between devices  11.5 us (4%)
  local copies, waits for them, and re-layouts  6.39 us (2%)
    psum x1, waiting for transfers between devices, local(): grad_hidden, grad_out = lax.psum((local_hidden, local_out), 'dev')  130 us
    all_to_all x1, waiting for transfers between devices, local(): lax.all_to_all(back.reshape(devices, rows, width), 'dev', split_axis=0, c...  25.2 us
    all_to_all x1, waiting for transfers between devices, local(): lax.all_to_all(payload, 'dev', split_axis=0, concat_axis=0, tiled=True)  23.1 us
    reduce_sum x1, other arithmetic, local(): send_target = jnp.sum(jnp.where(seated, target[:, None, :], 0), axis=2)  8.96 us
    all_to_all x1, starting transfers between devices, local(): lax.all_to_all(payload, 'dev', split_axis=0, concat_axis=0, tiled=True)  7.5 us
    reduce_sum x1, other arithmetic, owner(): jnp.sum(jnp.where(table_ids[:, None, :] == which, recip[:, None, :], 0.0)...  5.26 us
  transfers between devices with their start and end apart: 3, of which 3 were waited for; matrix products, arithmetic and copies ran while one was open for 4% of the time, Pallas kernels for 0%

profile of v1, /device:TPU:0, one launch (start us, length us, event | category | flops | bytes accessed | tf_op | source)
XLA Modules:
  0.0 255.2 jit_solution(18141052734242761697)
XLA Ops:
  7.2 0.0 copy-start
  7.2 0.0 copy-start.16
  7.2 1.4 select_reduce_fusion.1
  8.6 0.9 slice_add_fusion.4
  9.5 0.2 eq.168
  9.7 0.8 fusion.17
  10.5 0.0 copy-start.8
  10.5 0.3 select_select_fusion
  10.9 0.0 copy-done.16
  10.9 9.0 %fusion = s32[512,8]{1,0:T(8,128)S(1)} fusion(s32[512,512]{1,0:T(8,128)S(1)} %select_select_fusion, bf16[512,512]{1,0:T(8,128)(2,1)S(1)} %fusion.17, bf16[8]{0:T(256)(128)(2,1)S(1)} %iota_convert_fusion), kind=kLoop, calls=%fused_computation.4 | loop fusion | flops 6287360 | bytes 1589264 | tf_op jit(solution)/shard_map/reduce_sum | solution.py:107
  19.8 0.1 reshape.298
  20.1 0.0 copy-done
  20.1 0.0 copy-start.17
  20.1 3.0 %multiply_convert_fusion = (bf16[512,512]{1,0:T(8,128)(2,1)S(1)}, f32[512,512]{1,0:T(8,128)}) fusion(bf16[512,1024]{1,0:T(8,128)(2,1)S(1)} %copy-done, bf16[1024,512]{1,0:T(8,128)(2,1)} %param.10), kind=kOutput, calls=%fused_computation.57 | convolution fusion | flops 538181632 | bytes 3670016 | tf_op jit(solution)/shard_map/dot_general | solution.py:113
  23.1 0.0 copy-done.8
  23.1 0.0 copy-done.17
  23.1 2.2 fusion.4
  25.3 0.0 copy-done.6
  25.3 0.0 copy-start.4
  25.3 0.0 copy-start.3
  25.3 1.1 pad_maximum_fusion
  26.4 7.5 %all-to-all-start = ((bf16[32,144,128]{2,1,0:T(8,128)(2,1)}), bf16[32,144,128]{2,1,0:T(8,128)(2,1)S(1)}, u32[]{:S(2)}, u32[]{:S(2)}) async-start(bf16[32,144,128]{2,1,0:T(8,128)(2,1)} %pad_maximum_fusion), calls=%async_computation | async-start | bytes 2359296 | tf_op jit(solution)/shard_map/all_to_all | solution.py:118
  34.0 5.3 %select_reduce_fusion = f32[16,128]{1,0:T(8,128)S(1)} fusion(f32[16,4096]{1,0:T(8,128)S(1)} %convert_divide_fusion, s32[16,4096]{1,0:T(8,128)S(1)} %copy-done.3), kind=kLoop, calls=%fused_computation | loop fusion | flops 25163776 | bytes 532480 | tf_op jit(solution)/shard_map/reduce_sum | solution.py:43
  39.3 0.0 copy-start.10
  39.3 0.2 fusion.44
  39.6 0.1 copy.75
  39.6 23.1 %all-to-all-done = bf16[32,144,128]{2,1,0:T(8,128)(2,1)S(1)} async-done(((bf16[32,144,128]{2,1,0:T(8,128)(2,1)}), bf16[32,144,128]{2,1,0:T(8,128)(2,1)S(1)}, u32[]{:S(2)}, u32[]{:S(2)}) %all-to-all-start) | async-done | bytes 1179680 | tf_op jit(solution)/shard_map/all_to_all | solution.py:118
  62.8 0.1 copy.93
  62.9 0.1 copy.53
  63.0 0.1 copy.56
  63.1 0.1 copy.57
  63.2 0.0 copy-start.5
  63.2 1.4 select_reduce_fusion.4
  64.6 0.0 copy-done.1
  64.7 0.0 copy-start.12
  64.7 0.0 copy-done.5
  64.7 1.7 add_reduce_fusion
  66.4 1.0 select_reduce_fusion.2
  67.4 1.3 fusion.41
  68.6 0.0 copy-done.10
  68.6 0.0 copy-done.12
  68.7 1.3 fusion.15
  69.9 1.3 copy.92
  71.2 3.8 %all-to-all-start.1 = ((bf16[32,128,128]{2,1,0:T(8,128)(2,1)}), bf16[32,128,128]{2,1,0:T(8,128)(2,1)}, u32[]{:S(2)}, u32[]{:S(2)}) async-start(bf16[32,128,128]{2,1,0:T(8,128)(2,1)} %bitcast.84), calls=%async_computation.1 | async-start | bytes 2097152 | tf_op jit(solution)/shard_map/all_to_all | solution.py:133
  75.0 0.3 all-reduce.4.cloned.1.call-start
  75.2 0.1 copy.63
  75.3 0.1 copy.64
  75.5 0.1 copy.55
  75.6 0.1 copy.66
  75.7 0.1 copy.62
  75.8 0.1 copy.65
  75.9 25.2 %all-to-all-done.1 = bf16[32,128,128]{2,1,0:T(8,128)(2,1)} async-done(((bf16[32,128,128]{2,1,0:T(8,128)(2,1)}), bf16[32,128,128]{2,1,0:T(8,128)(2,1)}, u32[]{:S(2)}, u32[]{:S(2)}) %all-to-all-start.1) | async-done | bytes 1048608 | tf_op jit(solution)/shard_map/all_to_all | solution.py:133
  101.1 3.9 %fusion.18 = bf16[512,128]{1,0:T(8,128)(2,1)S(1)} fusion(bf16[4096,128]{1,0:T(8,128)(2,1)} %bitcast.27, bf16[512,512]{1,0:T(8,128)(2,1)} %copy-done.8, bf16[8]{0:T(256)(128)(2,1)} %copy-done.16), kind=kOutput, calls=%fused_computation.43 | convolution fusion | flops 539033600 | bytes 1703952 | tf_op jit(solution)/shard_map/dot_general | solution.py:136
  105.1 1.0 fusion.61
  106.1 3.6 %convolution_bitcast_fusion = f32[1024,512]{0,1:T(8,128)} fusion(bf16[512,1024]{1,0:T(8,128)(2,1)S(1)} %copy-done, bf16[512,128]{1,0:T(8,128)(2,1)S(1)} %fusion.18, bf16[512,128]{1,0:T(8,128)(2,1)} %param.11, f32[512,512]{1,0:T(8,128)} %get-tuple-element.45), kind=kOutput, calls=%fused_computation.28 | convolution fusion | flops 606339072 | bytes 4456448 | tf_op jit(solution)/shard_map/dot_general | solution.py:142
  109.8 0.0 all-reduce.4.cloned.1.call-update
  109.8 0.2 convert_reduce_fusion
  110.0 0.5 div.73
  110.5 0.0 copy-done.13
  110.5 2.2 fusion.20
  112.7 2.0 convolution_add_fusion
  114.8 130.0 %all-reduce.4.cloned.1.call-done = (f32[1024,512]{0,1:T(8,128)}, f32[512,128]{1,0:T(8,128)}) async-done(((f32[1024,512]{0,1:T(8,128)}, f32[512,128]{1,0:T(8,128)}), (f32[1024,512]{0,1:T(8,128)}, f32[512,128]{1,0:T(8,128)})) %all-reduce.4.cloned.1.call-update) | async-done | bytes 2359312 | tf_op jit(solution)/shard_map/psum | solution.py:143
  244.8 2.9 %copy.70 = f32[1024,512]{1,0:T(8,128)} copy(f32[1024,512]{0,1:T(8,128)} %get-tuple-element.27) | data formatting | bytes 4194304
  247.7 0.7 copy.96
  (34 shorter events, 0.3 us)
Async XLA Ops:
  7.2 12.9 %copy-start = (bf16[512,1024]{1,0:T(8,128)(2,1)S(1)}, bf16[512,1024]{1,0:T(8,128)(2,1)}, u32[]{:S(2)}) copy-start(bf16[512,1024]{1,0:T(8,128)(2,1)} %param.9) | copy-start | bytes 3145732
  7.2 3.7 %copy-start.16 = (bf16[8]{0:T(256)(128)(2,1)}, bf16[8]{0:T(256)(128)(2,1)S(1)}, u32[]{:S(2)}) copy-start(bf16[8]{0:T(256)(128)(2,1)S(1)} %iota_convert_fusion) | copy-start | bytes 52
  10.5 12.6 %copy-start.8 = (bf16[512,512]{1,0:T(8,128)(2,1)}, bf16[512,512]{1,0:T(8,128)(2,1)S(1)}, u32[]{:S(2)}) copy-start(bf16[512,512]{1,0:T(8,128)(2,1)S(1)} %fusion.17) | copy-start | bytes 1572868
  20.1 3.0 %copy-start.17 = (bf16[512,128]{1,0:T(8,128)(2,1)S(1)}, bf16[512,128]{1,0:T(8,128)(2,1)}, u32[]{:S(2)}) copy-start(bf16[512,128]{1,0:T(8,128)(2,1)} %param.11) | copy-start | bytes 393220
  23.1 2.2 copy-start.6
  25.3 8.6 %copy-start.4 = (s32[16,4096]{1,0:T(8,128)S(1)}, s32[16,4096]{1,0:T(8,128)}, u32[]{:S(2)}) copy-start(s32[16,4096]{1,0:T(8,128)} %param.16) | copy-start | bytes 786436
  25.3 8.7 %copy-start.3 = (s32[16,4096]{1,0:T(8,128)S(1)}, s32[16,4096]{1,0:T(8,128)}, u32[]{:S(2)}) copy-start(s32[16,4096]{1,0:T(8,128)} %param.15) | copy-start | bytes 786436
  26.4 36.3 %all-to-all-start = ((bf16[32,144,128]{2,1,0:T(8,128)(2,1)}), bf16[32,144,128]{2,1,0:T(8,128)(2,1)S(1)}, u32[]{:S(2)}, u32[]{:S(2)}) async-start(bf16[32,144,128]{2,1,0:T(8,128)(2,1)} %pad_maximum_fusion), calls=%async_computation | async-start | bytes 2359296 | tf_op jit(solution)/shard_map/all_to_all | solution.py:118
  39.3 29.4 %copy-start.10 = (f32[16,128]{1,0:T(8,128)}, f32[16,128]{1,0:T(8,128)S(1)}, u32[]{:S(2)}) copy-start(f32[16,128]{1,0:T(8,128)S(1)} %log.16) | copy-start | bytes 24580
  62.7 1.9 copy-start.1
  63.2 1.5 copy-start.5
  64.7 4.0 %copy-start.12 = (s32[16,256]{1,0:T(8,128)}, s32[16,256]{1,0:T(8,128)S(1)}, u32[]{:S(2)}) copy-start(s32[16,256]{1,0:T(8,128)S(1)} %convert_select_fusion) | copy-start | bytes 49156
  67.4 8.1 %copy-start.14 = (f32[16,256]{1,0:T(8,128)}, f32[16,256]{1,0:T(8,128)S(1)}, u32[]{:S(2)}) copy-start(f32[16,256]{1,0:T(8,128)S(1)} %get-tuple-element.21) | copy-start | bytes 49156
  71.2 29.9 %all-to-all-start.1 = ((bf16[32,128,128]{2,1,0:T(8,128)(2,1)}), bf16[32,128,128]{2,1,0:T(8,128)(2,1)}, u32[]{:S(2)}, u32[]{:S(2)}) async-start(bf16[32,128,128]{2,1,0:T(8,128)(2,1)} %bitcast.84), calls=%async_computation.1 | async-start | bytes 2097152 | tf_op jit(solution)/shard_map/all_to_all | solution.py:133
  75.0 169.8 %all-reduce.4.cloned.1.call-start = ((), (), s32[]{:S(2)}) async-start(), calls=%async_computation.2 | async-start | bytes 4718592 | tf_op jit(solution)/shard_map/psum | solution.py:143
  101.1 3.9 %copy-start.7 = (bf16[512,512]{1,0:T(8,128)(2,1)S(1)}, bf16[512,512]{1,0:T(8,128)(2,1)}, u32[]{:S(2)}) copy-start(bf16[512,512]{1,0:T(8,128)(2,1)} %copy-done.6) | copy-start | bytes 1572868
  109.8 0.8 copy-start.11
  109.8 0.8 copy-start.13
  109.8 0.8 copy-start.15
  110.5 2.2 copy-start.2
  244.8 2.9 %copy-start.9 = (f32[512,128]{1,0:T(8,128)S(1)}, f32[512,128]{1,0:T(8,128)}, u32[]{:S(2)}) copy-start(f32[512,128]{1,0:T(8,128)} %get-tuple-element.50) | copy-start | bytes 786436
Sparse Core Ops, SparseCore 0:
  109.9 134.7 all-reduce.3

commit v2 on v1

--- a/solution.py
+++ b/solution.py
@@ -1,6 +1,10 @@
+import functools
+
 import jax
 import jax.numpy as jnp
 from jax import lax
+from jax.experimental import pallas as pl
+from jax.experimental.pallas import tpu as pltpu
 from jax.sharding import PartitionSpec as P
 
 
@@ -87,6 +91,142 @@
     dquery = both("cqi,cie->cqe", block_items).astype(jnp.bfloat16)
     dtable = both("cqi,cqe->cie", queries)
     return cluster_loss, dquery, dtable
+
+
+LANES = 3
+
+
+def bit_orders(bits):
+    turn = [b for b in (1, 2, 3) if b < bits]
+    rest = [b for b in range(bits) if b > 3]
+    orders = []
+    for lane in range(LANES):
+        k = lane % max(1, len(turn))
+        orders.append([0] + turn[k:] + turn[:k] + rest)
+    return orders
+
+
+def blocks_of(ref):
+    rows, columns = ref.shape
+    return [(c, rows) for c in range(columns // 128)]
+
+
+def reduce_kernel(bits, unit, big_ref, small_ref, big_out, small_out, acc, out, inbox, full, send, recv):
+    me = lax.axis_index("dev")
+    mesh = pl.DeviceIdType.MESH
+    orders = bit_orders(bits)
+    per_lane = unit << bits
+    partners = [me + (1 << b) * (1 - 2 * ((me // (1 << b)) % 2)) for b in range(bits)]
+    bit = [(me // (1 << b)) % 2 for b in range(bits)]
+
+    barrier = pltpu.get_barrier_semaphore()
+    for b in range(bits):
+        pl.semaphore_signal(barrier, inc=1, device_id=(partners[b],), device_id_type=mesh)
+    row = 0
+    for ref in (big_ref, small_ref):
+        for c, rows in blocks_of(ref):
+            acc[row : row + rows, :] = ref[:, c * 128 : (c + 1) * 128]
+            row += rows
+    if row < LANES * per_lane:
+        acc[row:, :] = jnp.zeros((LANES * per_lane - row, 128), jnp.float32)
+
+    off = [lane * per_lane for lane in range(LANES)]
+    length = per_lane
+    gap = []
+    at = 0
+    for s in range(bits):
+        gap.append(at)
+        at += per_lane >> (s + 1)
+    started = []
+
+    def rows_at(first, count):
+        return pl.ds(pl.multiple_of(first, 16), count)
+
+    for s in range(bits):
+        half = length // 2
+        copies = []
+        for lane in range(LANES):
+            b = orders[lane][s]
+            give = off[lane] + (1 - bit[b]) * half
+            off[lane] = off[lane] + bit[b] * half
+            out[rows_at(give, half), :] = acc[rows_at(give, half), :].astype(jnp.bfloat16)
+            if s == 0 and lane == 0:
+                pl.semaphore_wait(barrier, bits)
+            copy = pltpu.make_async_remote_copy(
+                src_ref=out.at[rows_at(give, half), :],
+                dst_ref=inbox.at[pl.ds(lane * per_lane + gap[s], half), :],
+                send_sem=send.at[lane, s],
+                recv_sem=recv.at[lane, s],
+                device_id=(partners[b],),
+                device_id_type=mesh,
+            )
+            copy.start()
+            copies.append(copy)
+            started.append(copy)
+        for lane in range(LANES):
+            copies[lane].wait_recv()
+            kept = rows_at(off[lane], half)
+            got = inbox[pl.ds(lane * per_lane + gap[s], half), :].astype(jnp.float32)
+            acc[kept, :] = acc[kept, :] + got
+        length = half
+    for lane in range(LANES):
+        kept = rows_at(off[lane], length)
+        full[kept, :] = acc[kept, :].astype(jnp.bfloat16)
+    for s in range(bits - 1, -1, -1):
+        copies = []
+        for lane in range(LANES):
+            b = orders[lane][s]
+            held = rows_at(off[lane], length)
+            copy = pltpu.make_async_remote_copy(
+                src_ref=full.at[held, :],
+                dst_ref=full.at[held, :],
+                send_sem=send.at[lane, bits + s],
+                recv_sem=recv.at[lane, bits + s],
+                device_id=(partners[b],),
+                device_id_type=mesh,
+            )
+            copy.start()
+            copies.append(copy)
+            started.append(copy)
+            off[lane] = off[lane] - bit[b] * length
+        for lane in range(LANES):
+            copies[lane].wait_recv()
+        length = length * 2
+    for copy in started:
+        copy.wait_send()
+    row = 0
+    for ref in (big_out, small_out):
+        for c, rows in blocks_of(ref):
+            ref[:, c * 128 : (c + 1) * 128] = full[row : row + rows, :]
+            row += rows
+
+
+def sum_over_devices(big, small):
+    devices = lax.axis_size("dev")
+    bits = devices.bit_length() - 1
+    total = (big.size + small.size) // 128
+    unit = -(-total // (LANES * devices * 16)) * 16
+    rows = LANES * devices * unit
+    summed = pl.pallas_call(
+        functools.partial(reduce_kernel, bits, unit),
+        out_shape=(
+            jax.ShapeDtypeStruct(big.shape, jnp.bfloat16),
+            jax.ShapeDtypeStruct(small.shape, jnp.bfloat16),
+        ),
+        in_specs=[pl.BlockSpec(memory_space=pltpu.VMEM)] * 2,
+        out_specs=[pl.BlockSpec(memory_space=pltpu.VMEM)] * 2,
+        scratch_shapes=[
+            pltpu.VMEM((rows, 128), jnp.float32),
+            pltpu.VMEM((rows, 128), jnp.bfloat16),
+            pltpu.VMEM((rows, 128), jnp.bfloat16),
+            pltpu.VMEM((rows, 128), jnp.bfloat16),
+            pltpu.SemaphoreType.DMA((LANES, 2 * bits)),
+            pltpu.SemaphoreType.DMA((LANES, 2 * bits)),
+        ],
+        compiler_params=pltpu.CompilerParams(collective_id=0, has_side_effects=True),
+        name="sum_over_devices",
+    )(big, small)
+    return tuple(part.astype(jnp.float32) for part in summed)
 
 
 def local(
@@ -140,7 +280,7 @@
     dhidden = jnp.dot(dq_total, w_out.T, preferred_element_type=jnp.float32)
     dpre = (dhidden * silu_grad(pre)).astype(jnp.bfloat16)
     local_hidden = jnp.dot(features.T, dpre, preferred_element_type=jnp.float32)
-    grad_hidden, grad_out = lax.psum((local_hidden, local_out), "dev")
+    grad_hidden, grad_out = sum_over_devices(local_hidden, local_out)
     return (slot_loss, grad_hidden, grad_out, dtable.reshape(items.shape[0], width))
 
 

time: 256 us -> 142 us (0.55)
  waiting for transfers between devices: 178 us -> 43.3 us
  Pallas kernels: 0 us -> 34.9 us
  between operations: 14.5 us -> 1.14 us
  other arithmetic: 20.1 us -> 24.5 us
  local copies, waits for them, and re-layouts: 6.39 us -> 2.8 us
    psum x1 -> x0, waiting for transfers between devices: 130 us -> none  [local(): grad_hidden, grad_out = lax.psum((local_hidden, local_out), 'dev')]
    pallas_call x0 -> x1, Pallas kernels: none -> 34.9 us  [sum_over_devices(): pl.pallas_call(functools.partial(reduce_kernel, bits, unit), out_shape=(j...]
    all_to_all x1, waiting for transfers between devices: 25.2 us -> 20.2 us  [local(): lax.all_to_all(back.reshape(devices, rows, width), 'dev', split_axis=0, c...]
    convert_element_type x0 -> x2, other arithmetic: none -> 4.46 us  [sum_over_devices(): return tuple((part.astype(jnp.float32) for part in summed))]
    unnamed x41 -> x43, local copies, waits for them, and re-layouts: 3.87 us -> 0.26 us
  transfers between devices with their start and end apart: 3 -> 2, of which waited for: 3 -> 2; matrix products, arithmetic and copies ran while one was open for 4% -> 8% of each run, Pallas kernels for 0% -> 0%
where the time goes in v2:
time: 142 us; the launch traced here: 141 us
  waiting for transfers between devices  43.3 us (30%)
  Pallas kernels  34.9 us (25%)
  other arithmetic  24.5 us (17%)
  matrix products  23.2 us (16%)
  starting transfers between devices  11.5 us (8%)
  local copies, waits for them, and re-layouts  2.8 us (2%)
    pallas_call x1, Pallas kernels, sum_over_devices(): pl.pallas_call(functools.partial(reduce_kernel, bits, unit), out_shape=(j...  34.9 us
    all_to_all x1, waiting for transfers between devices, local(): lax.all_to_all(payload, 'dev', split_axis=0, concat_axis=0, tiled=True)  23.1 us
    all_to_all x1, waiting for transfers between devices, local(): lax.all_to_all(back.reshape(devices, rows, width), 'dev', split_axis=0, c...  20.2 us
    reduce_sum x1, other arithmetic, local(): send_target = jnp.sum(jnp.where(seated, target[:, None, :], 0), axis=2)  8.96 us
    all_to_all x1, starting transfers between devices, local(): lax.all_to_all(payload, 'dev', split_axis=0, concat_axis=0, tiled=True)  7.51 us
    reduce_sum x1, other arithmetic, owner(): jnp.sum(jnp.where(table_ids[:, None, :] == which, recip[:, None, :], 0.0)...  5.26 us
    convert_element_type x2, other arithmetic, sum_over_devices(): return tuple((part.astype(jnp.float32) for part in summed))  4.46 us
    dot_general x1, matrix products, local(): lax.dot_general(select, returned, (((0,), (0,)), ((), ())), preferred_ele...  3.97 us
  transfers between devices with their start and end apart: 2, of which 2 were waited for; matrix products, arithmetic and copies ran while one was open for 8% of the time, Pallas kernels for 0%

profile of v2, /device:TPU:0, one launch (start us, length us, event | category | flops | bytes accessed | tf_op | source)
XLA Modules:
  0.0 141.4 jit_solution(16883549128718815108)
XLA Ops:
  0.6 0.0 copy-start
  0.7 0.0 copy-start.15
  0.7 1.4 select_reduce_fusion.1
  2.1 0.9 slice_add_fusion.4
  3.0 0.2 eq.168
  3.1 0.8 fusion.17
  4.0 0.0 copy-start.8
  4.0 0.3 select_select_fusion
  4.3 0.0 copy-done.15
  4.3 9.0 %fusion = s32[512,8]{1,0:T(8,128)S(1)} fusion(s32[512,512]{1,0:T(8,128)S(1)} %select_select_fusion, bf16[512,512]{1,0:T(8,128)(2,1)S(1)} %fusion.17, bf16[8]{0:T(256)(128)(2,1)S(1)} %iota_convert_fusion), kind=kLoop, calls=%fused_computation.4 | loop fusion | flops 6287360 | bytes 1589264 | tf_op jit(solution)/shard_map/reduce_sum | solution.py:247
  13.3 0.1 reshape.298
  13.5 0.0 copy-done
  13.5 0.0 copy-start.17
  13.5 3.0 %multiply_convert_fusion = (bf16[512,512]{1,0:T(8,128)(2,1)S(1)}, f32[512,512]{1,0:T(8,128)}) fusion(bf16[512,1024]{1,0:T(8,128)(2,1)S(1)} %copy-done, bf16[1024,512]{1,0:T(8,128)(2,1)} %param.10), kind=kOutput, calls=%fused_computation.57 | convolution fusion | flops 538181632 | bytes 3670016 | tf_op jit(solution)/shard_map/dot_general | solution.py:253
  16.6 0.0 copy-done.8
  16.6 0.0 copy-done.17
  16.6 2.2 %fusion.4 = bf16[4096,128]{1,0:T(8,128)(2,1)S(1)} fusion(bf16[4096]{0:T(1024)(128)(2,1)S(1)} %eq.168, bf16[512,512]{1,0:T(8,128)(2,1)S(1)} %fusion.17, bf16[512,512]{1,0:T(8,128)(2,1)S(1)} %get-tuple-element.30, bf16[512,128]{1,0:T(8,128)(2,1)S(1)} %copy-done.17), kind=kOutput, calls=%fused_computation.8 | convolution fusion | flops 606666752 | bytes 2236416 | tf_op jit(solution)/shard_map/dot_general | solution.py:256
  18.7 0.0 copy-done.6
  18.7 0.0 copy-start.4
  18.7 0.0 copy-start.3
  18.8 1.1 pad_maximum_fusion
  19.9 7.5 %all-to-all-start = ((bf16[32,144,128]{2,1,0:T(8,128)(2,1)}), bf16[32,144,128]{2,1,0:T(8,128)(2,1)S(1)}, u32[]{:S(2)}, u32[]{:S(2)}) async-start(bf16[32,144,128]{2,1,0:T(8,128)(2,1)} %pad_maximum_fusion), calls=%async_computation | async-start | bytes 2359296 | tf_op jit(solution)/shard_map/all_to_all | solution.py:258
  27.4 0.0 copy-done.4
  27.4 0.0 copy-done.3
  27.5 5.3 %select_reduce_fusion = f32[16,128]{1,0:T(8,128)S(1)} fusion(f32[16,4096]{1,0:T(8,128)S(1)} %convert_divide_fusion, s32[16,4096]{1,0:T(8,128)S(1)} %copy-done.3), kind=kLoop, calls=%fused_computation | loop fusion | flops 25163776 | bytes 532480 | tf_op jit(solution)/shard_map/reduce_sum | solution.py:47
  32.7 0.0 copy-start.9
  32.7 0.2 fusion.44
  33.0 0.1 copy.76
  33.1 23.1 %all-to-all-done = bf16[32,144,128]{2,1,0:T(8,128)(2,1)S(1)} async-done(((bf16[32,144,128]{2,1,0:T(8,128)(2,1)}), bf16[32,144,128]{2,1,0:T(8,128)(2,1)S(1)}, u32[]{:S(2)}, u32[]{:S(2)}) %all-to-all-start) | async-done | bytes 1179680 | tf_op jit(solution)/shard_map/all_to_all | solution.py:258
  56.2 0.1 copy.94
  56.3 0.1 copy.53
  56.4 0.1 copy.56
  56.6 0.1 copy.57
  56.7 0.0 copy-start.5
  56.7 1.4 select_reduce_fusion.4
  58.1 0.0 copy-done.1
  58.1 0.0 copy-start.11
  58.1 1.7 %add_reduce_fusion = (f32[16,256]{1,0:T(8,128)S(1)}, f32[16,256,128]{1,2,0:T(8,128)S(1)}) fusion(f32[16,128]{1,0:T(8,128)S(1)} %log.16, bf16[16,128,128]{2,1,0:T(8,128)(2,1)S(1)} %bitcast.88, bf16[32,144,128]{2,1,0:T(8,128)(2,1)} %copy-done.1), kind=kOutput, calls=%fused_computation.26 | convolution fusion | flops 135262208 | bytes 3694592 | tf_op jit(solution)/shard_map/cqe,cie->cqi/dot_general | solution.py:67
  59.8 1.0 select_reduce_fusion.2
  60.8 0.0 copy-start.13
  60.8 1.3 fusion.41
  62.1 0.0 copy-done.9
  62.1 0.0 copy-done.11
  62.1 1.3 fusion.15
  63.4 1.3 copy.93
  64.7 4.0 %all-to-all-start.1 = ((bf16[32,128,128]{2,1,0:T(8,128)(2,1)}), bf16[32,128,128]{2,1,0:T(8,128)(2,1)}, u32[]{:S(2)}, u32[]{:S(2)}) async-start(bf16[32,128,128]{2,1,0:T(8,128)(2,1)} %bitcast.84), calls=%async_computation.1 | async-start | bytes 2097152 | tf_op jit(solution)/shard_map/all_to_all | solution.py:273
  68.7 0.1 copy.63
  68.8 0.1 copy.64
  68.9 0.1 copy.55
  69.0 0.1 copy.66
  69.1 0.1 copy.62
  69.2 0.1 copy.65
  69.4 0.2 convert_reduce_fusion
  69.6 0.5 div.73
  70.1 2.2 %fusion.20 = f32[16,128,128]{2,1,0:T(8,128)S(1)} fusion(f32[16,256,128]{1,2,0:T(8,128)S(1)} %get-tuple-element.33, f32[16,256]{1,0:T(8,128)} %copy-done.13, s32[16,256]{1,0:T(8,128)} %copy-done.11, f32[16,256]{1,0:T(8,128)S(1)} %get-tuple-element.32, f32[16,128]{1,0:T(8,128)} %copy-done.9, bf16[32,144,128]{2,1,0:T(8,128)(2,1)} %copy-done.1), kind=kOutput, calls=%fused_computation.46 | convolution fusion | flops 138412032 | bytes 4251648 | tf_op jit(solution)/shard_map/cqi,cqe->cie/dot_general | solution.py:87
  72.4 2.0 %convolution_add_fusion = f32[16,128,128]{2,1,0:T(8,128)} fusion(f32[16,128,128]{2,1,0:T(8,128)S(1)} %fusion.20, f32[16,256,128]{1,2,0:T(8,128)S(1)} %get-tuple-element.33, f32[16,256]{1,0:T(8,128)S(1)} %copy-done.14, s32[16,256]{1,0:T(8,128)S(1)} %copy-done.12, f32[16,256]{1,0:T(8,128)S(1)} %get-tuple-element.32, f32[16,128]{1,0:T(8,128)S(1)} %copy-done.10, ...), kind=kOutput, calls=%fused_computation.37 | convolution fusion | flops 139198464 | bytes 5300224 | tf_op jit(solution)/shard_map/cqi,cqe->cie/dot_general | solution.py:89
  74.4 20.2 %all-to-all-done.1 = bf16[32,128,128]{2,1,0:T(8,128)(2,1)} async-done(((bf16[32,128,128]{2,1,0:T(8,128)(2,1)}), bf16[32,128,128]{2,1,0:T(8,128)(2,1)}, u32[]{:S(2)}, u32[]{:S(2)}) %all-to-all-start.1) | async-done | bytes 1048608 | tf_op jit(solution)/shard_map/all_to_all | solution.py:273
  94.6 4.0 %fusion.18 = bf16[512,128]{1,0:T(8,128)(2,1)S(1)} fusion(bf16[4096,128]{1,0:T(8,128)(2,1)} %bitcast.27, bf16[512,512]{1,0:T(8,128)(2,1)} %copy-done.8, bf16[8]{0:T(256)(128)(2,1)S(1)} %copy-done.16), kind=kOutput, calls=%fused_computation.43 | convolution fusion | flops 539033600 | bytes 1703952 | tf_op jit(solution)/shard_map/dot_general | solution.py:276
  98.6 1.0 fusion.61.small_ref
  99.7 0.0 copy-done.19
  99.7 2.3 %convolution_bitcast_fusion.big_ref = f32[1024,512]{1,0:T(8,128)} fusion(bf16[512,1024]{1,0:T(8,128)(2,1)S(1)} %copy-done, bf16[512,128]{1,0:T(8,128)(2,1)S(1)} %fusion.18, bf16[512,128]{1,0:T(8,128)(2,1)S(1)} %copy-done.18, f32[512,512]{1,0:T(8,128)S(1)} %copy-done.19), kind=kOutput, calls=%fused_computation.28 | convolution fusion | flops 606339072 | bytes 4456448 | tf_op jit(solution)/shard_map/dot_general | solution.py:282
  102.0 34.9 %sum_over_devices.1 = (bf16[1024,512]{1,0:T(8,128)(2,1)}, bf16[512,128]{1,0:T(8,128)(2,1)}) custom-call(f32[1024,512]{1,0:T(8,128)} %convolution_bitcast_fusion.big_ref, f32[512,128]{1,0:T(8,128)} %fusion.61.small_ref), custom_call_target="tpu_custom_call" | custom-call | tf_op jit(solution)/shard_map/sum_over_devices/pallas_call | solution.py:210
  136.9 1.6 %convert_element_type.93 = f32[512,128]{1,0:T(8,128)} convert(bf16[512,128]{1,0:T(8,128)(2,1)} %get-tuple-element.7) | non-fusion elementwise | flops 65536 | bytes 393216 | tf_op jit(solution)/shard_map/convert_element_type | solution.py:229
  138.5 2.8 %convert_element_type.92 = f32[1024,512]{1,0:T(8,128)} convert(bf16[1024,512]{1,0:T(8,128)(2,1)} %get-tuple-element.6) | non-fusion elementwise | flops 524288 | bytes 3145728 | tf_op jit(solution)/shard_map/convert_element_type | solution.py:229
  (36 shorter events, 0.3 us)
Async XLA Ops:
  0.6 12.9 %copy-start = (bf16[512,1024]{1,0:T(8,128)(2,1)S(1)}, bf16[512,1024]{1,0:T(8,128)(2,1)}, u32[]{:S(2)}) copy-start(bf16[512,1024]{1,0:T(8,128)(2,1)} %param.9) | copy-start | bytes 3145732
  0.7 3.7 %copy-start.15 = (bf16[8]{0:T(256)(128)(2,1)}, bf16[8]{0:T(256)(128)(2,1)S(1)}, u32[]{:S(2)}) copy-start(bf16[8]{0:T(256)(128)(2,1)S(1)} %iota_convert_fusion) | copy-start | bytes 52
  4.0 12.6 %copy-start.8 = (bf16[512,512]{1,0:T(8,128)(2,1)}, bf16[512,512]{1,0:T(8,128)(2,1)S(1)}, u32[]{:S(2)}) copy-start(bf16[512,512]{1,0:T(8,128)(2,1)S(1)} %fusion.17) | copy-start | bytes 1572868
  13.5 3.0 %copy-start.17 = (bf16[512,128]{1,0:T(8,128)(2,1)S(1)}, bf16[512,128]{1,0:T(8,128)(2,1)}, u32[]{:S(2)}) copy-start(bf16[512,128]{1,0:T(8,128)(2,1)} %param.11) | copy-start | bytes 393220
  16.6 2.2 %copy-start.6 = (bf16[512,512]{1,0:T(8,128)(2,1)}, bf16[512,512]{1,0:T(8,128)(2,1)S(1)}, u32[]{:S(2)}) copy-start(bf16[512,512]{1,0:T(8,128)(2,1)S(1)} %get-tuple-element.30) | copy-start | bytes 1572868
  18.7 8.6 %copy-start.4 = (s32[16,4096]{1,0:T(8,128)S(1)}, s32[16,4096]{1,0:T(8,128)}, u32[]{:S(2)}) copy-start(s32[16,4096]{1,0:T(8,128)} %param.16) | copy-start | bytes 786436
  18.7 8.7 %copy-start.3 = (s32[16,4096]{1,0:T(8,128)S(1)}, s32[16,4096]{1,0:T(8,128)}, u32[]{:S(2)}) copy-start(s32[16,4096]{1,0:T(8,128)} %param.15) | copy-start | bytes 786436
  19.9 36.3 %all-to-all-start = ((bf16[32,144,128]{2,1,0:T(8,128)(2,1)}), bf16[32,144,128]{2,1,0:T(8,128)(2,1)S(1)}, u32[]{:S(2)}, u32[]{:S(2)}) async-start(bf16[32,144,128]{2,1,0:T(8,128)(2,1)} %pad_maximum_fusion), calls=%async_computation | async-start | bytes 2359296 | tf_op jit(solution)/shard_map/all_to_all | solution.py:258
  32.7 29.4 %copy-start.9 = (f32[16,128]{1,0:T(8,128)}, f32[16,128]{1,0:T(8,128)S(1)}, u32[]{:S(2)}) copy-start(f32[16,128]{1,0:T(8,128)S(1)} %log.16) | copy-start | bytes 24580
  56.2 1.9 %copy-start.1 = (bf16[32,144,128]{2,1,0:T(8,128)(2,1)}, bf16[32,144,128]{2,1,0:T(8,128)(2,1)S(1)}, u32[]{:S(2)}) copy-start(bf16[32,144,128]{2,1,0:T(8,128)(2,1)S(1)} %all-to-all-done) | copy-start | bytes 3538948
  56.7 1.5 %copy-start.5 = (bf16[2048,128]{1,0:T(8,128)(2,1)S(1)}, bf16[2048,128]{1,0:T(8,128)(2,1)}, u32[]{:S(2)}) copy-start(bf16[2048,128]{1,0:T(8,128)(2,1)} %param.12) | copy-start | bytes 1572868
  58.1 4.0 %copy-start.11 = (s32[16,256]{1,0:T(8,128)}, s32[16,256]{1,0:T(8,128)S(1)}, u32[]{:S(2)}) copy-start(s32[16,256]{1,0:T(8,128)S(1)} %convert_select_fusion) | copy-start | bytes 49156
  60.8 8.1 %copy-start.13 = (f32[16,256]{1,0:T(8,128)}, f32[16,256]{1,0:T(8,128)S(1)}, u32[]{:S(2)}) copy-start(f32[16,256]{1,0:T(8,128)S(1)} %get-tuple-element.9) | copy-start | bytes 49156
  64.7 29.9 %all-to-all-start.1 = ((bf16[32,128,128]{2,1,0:T(8,128)(2,1)}), bf16[32,128,128]{2,1,0:T(8,128)(2,1)}, u32[]{:S(2)}, u32[]{:S(2)}) async-start(bf16[32,128,128]{2,1,0:T(8,128)(2,1)} %bitcast.84), calls=%async_computation.1 | async-start | bytes 2097152 | tf_op jit(solution)/shard_map/all_to_all | solution.py:273
  70.1 2.3 %copy-start.2 = (bf16[32,144,128]{2,1,0:T(8,128)(2,1)S(1)}, bf16[32,144,128]{2,1,0:T(8,128)(2,1)}, u32[]{:S(2)}) copy-start(bf16[32,144,128]{2,1,0:T(8,128)(2,1)} %copy-done.1) | copy-start | bytes 3538948
  70.1 2.3 %copy-start.10 = (f32[16,128]{1,0:T(8,128)S(1)}, f32[16,128]{1,0:T(8,128)}, u32[]{:S(2)}) copy-start(f32[16,128]{1,0:T(8,128)} %copy-done.9) | copy-start | bytes 24580
  70.1 2.3 %copy-start.12 = (s32[16,256]{1,0:T(8,128)S(1)}, s32[16,256]{1,0:T(8,128)}, u32[]{:S(2)}) copy-start(s32[16,256]{1,0:T(8,128)} %copy-done.11) | copy-start | bytes 49156
  70.1 2.3 %copy-start.14 = (f32[16,256]{1,0:T(8,128)S(1)}, f32[16,256]{1,0:T(8,128)}, u32[]{:S(2)}) copy-start(f32[16,256]{1,0:T(8,128)} %copy-done.13) | copy-start | bytes 49156
  72.4 22.2 %copy-start.16 = (bf16[8]{0:T(256)(128)(2,1)S(1)}, bf16[8]{0:T(256)(128)(2,1)}, u32[]{:S(2)}) copy-start(bf16[8]{0:T(256)(128)(2,1)} %copy-done.15) | copy-start | bytes 52
  94.6 4.0 %copy-start.7 = (bf16[512,512]{1,0:T(8,128)(2,1)S(1)}, bf16[512,512]{1,0:T(8,128)(2,1)}, u32[]{:S(2)}) copy-start(bf16[512,512]{1,0:T(8,128)(2,1)} %copy-done.6) | copy-start | bytes 1572868
  94.6 5.0 %copy-start.18 = (bf16[512,128]{1,0:T(8,128)(2,1)S(1)}, bf16[512,128]{1,0:T(8,128)(2,1)}, u32[]{:S(2)}) copy-start(bf16[512,128]{1,0:T(8,128)(2,1)} %param.11) | copy-start | bytes 393220
  94.6 5.0 %copy-start.19 = (f32[512,512]{1,0:T(8,128)S(1)}, f32[512,512]{1,0:T(8,128)}, u32[]{:S(2)}) copy-start(f32[512,512]{1,0:T(8,128)} %get-tuple-element.31) | copy-start | bytes 3145732

commit v3 on v2

--- a/solution.py
+++ b/solution.py
@@ -13,7 +13,7 @@
     return sig * (1.0 + value * (1.0 - sig))
 
 
-def slot_codes(routes_t, positives_t, cluster_slot, capacity):
+def slot_codes(routes_t, positives, cluster_slot, capacity):
     visits, users = routes_t.shape
     clusters = cluster_slot.shape[0]
     ids = lax.broadcasted_iota(jnp.int32, (visits, clusters, users), 1)
@@ -21,22 +21,34 @@
         jnp.where(routes_t[:, None, :] == ids, cluster_slot[None, :, None], 0), axis=1
     )
     rows = lax.broadcasted_iota(jnp.int32, (clusters, users), 0)
+    columns = lax.broadcasted_iota(jnp.int32, (users, clusters), 1)
+    slots_u = slots.T
     member = jnp.zeros((clusters, users), jnp.bool_)
-    target = jnp.zeros((clusters, users), jnp.int32)
+    member_u = jnp.zeros((users, clusters), jnp.bool_)
+    target_u = jnp.zeros((users, clusters), jnp.int32)
     for r in range(visits):
-        same = slots[r][None, :] == rows
-        member = member | same
-        target = jnp.where(same, positives_t[r][None, :] + 1, target)
-    earlier = lax.broadcasted_iota(jnp.int32, (users, users), 0) < lax.broadcasted_iota(
-        jnp.int32, (users, users), 1
-    )
+        member = member | (slots[r][None, :] == rows)
+        same = slots_u[:, r][:, None] == columns
+        member_u = member_u | same
+        target_u = jnp.where(same, positives[:, r][:, None] + 1, target_u)
+    first = lax.broadcasted_iota(jnp.int32, (users, users), 0)
+    second = lax.broadcasted_iota(jnp.int32, (users, users), 1)
     rank = jnp.dot(
         member.astype(jnp.bfloat16),
-        earlier.astype(jnp.bfloat16),
+        (first < second).astype(jnp.bfloat16),
         preferred_element_type=jnp.float32,
     )
+    rank_u = jnp.dot(
+        (second < first).astype(jnp.bfloat16),
+        member_u.astype(jnp.bfloat16),
+        preferred_element_type=jnp.float32,
+    )
     code = jnp.where(member, rank, -1.0).astype(jnp.bfloat16)
-    return code, target
+    code_u = jnp.where(member_u, rank_u, -1.0)
+    seats = [
+        jnp.sum(jnp.where(code_u == k, target_u, 0), axis=0) for k in range(capacity)
+    ]
+    return code, jnp.stack(seats)
 
 
 def owner(queries, targets, block_items, table_ids, counts):
@@ -240,14 +252,14 @@
     item_rows = items.shape[0] // local_clusters
     capacity = max(2, 2 * users * visits // (local_clusters * devices))
     rows = local_clusters * capacity
-    code, target = slot_codes(routes.T, positives.T, cluster_slot, capacity)
+    code, send_target = slot_codes(routes.T, positives, cluster_slot, capacity)
     seats = lax.broadcasted_iota(jnp.int32, (1, capacity, 1), 1).astype(jnp.bfloat16)
     seated = code[:, None, :] == seats
     select = seated.astype(jnp.bfloat16).reshape(clusters * capacity, users)
-    send_target = jnp.sum(jnp.where(seated, target[:, None, :], 0), axis=2)
-    send_target = send_target.reshape(devices, rows)
+    send_target = send_target.reshape(capacity, devices, local_clusters)
+    send_target = send_target.transpose(1, 0, 2).reshape(devices, rows)
     coded = jnp.concatenate([send_target // 64, send_target % 64], axis=1)
-    extra = -(-coded.shape[1] // (16 * width)) * 16
+    extra = -(-coded.shape[1] // (8 * width)) * 8
     coded = jnp.pad(coded, ((0, 0), (0, extra * width - coded.shape[1])))
     coded = coded.astype(jnp.bfloat16).reshape(devices, extra, width)
     pre = jnp.dot(features, w_hidden, preferred_element_type=jnp.float32)
@@ -260,8 +272,8 @@
     got_query = got_query.transpose(1, 0, 2, 3).reshape(local_clusters, devices * capacity, width)
     got_coded = got[:, rows:].reshape(devices, extra * width).astype(jnp.int32)
     got_target = got_coded[:, :rows] * 64 + got_coded[:, rows : 2 * rows] - 1
-    got_target = got_target.reshape(devices, local_clusters, capacity)
-    got_target = got_target.transpose(1, 0, 2).reshape(local_clusters, devices * capacity)
+    got_target = got_target.reshape(devices, capacity, local_clusters)
+    got_target = got_target.transpose(2, 0, 1).reshape(local_clusters, devices * capacity)
     slot_loss, dquery, dtable = owner(
         got_query,
         got_target,

time: 142 us -> 134 us (0.944)
  other arithmetic: 24.5 us -> 15.2 us
  matrix products: 23.2 us -> 25.3 us
    reduce_sum x1 -> x0, other arithmetic: 8.96 us -> none  [local(): send_target = jnp.sum(jnp.where(seated, target[:, None, :], 0), axis=2)]
    dot_general x1 -> x2, matrix products: 0.85 us -> 2.93 us  [the longest x1 2.09 us: slot_codes(): jnp.dot((second < first).astype(jnp.bfloat16), member_u.astype(jnp.bfloat...]
where the time goes in v3:
time: 134 us
  waiting for transfers between devices  42 us (31%)
  Pallas kernels  34.9 us (26%)
  matrix products  25.3 us (19%)
  other arithmetic  15.2 us (11%)
  starting transfers between devices  11.5 us (9%)
  local copies, waits for them, and re-layouts  3.48 us (3%)
    pallas_call x1, Pallas kernels, sum_over_devices(): pl.pallas_call(functools.partial(reduce_kernel, bits, unit), out_shape=(j...  34.9 us
    all_to_all x1, waiting for transfers between devices, local(): lax.all_to_all(payload, 'dev', split_axis=0, concat_axis=0, tiled=True)  21.7 us
    all_to_all x1, waiting for transfers between devices, local(): lax.all_to_all(back.reshape(devices, rows, width), 'dev', split_axis=0, c...  20.3 us
    all_to_all x1, starting transfers between devices, local(): lax.all_to_all(payload, 'dev', split_axis=0, concat_axis=0, tiled=True)  7.51 us
    reduce_sum x1, other arithmetic, owner(): jnp.sum(jnp.where(table_ids[:, None, :] == which, recip[:, None, :], 0.0)...  5.26 us
    convert_element_type x2, other arithmetic, sum_over_devices(): return tuple((part.astype(jnp.float32) for part in summed))  4.46 us
    all_to_all x1, starting transfers between devices, local(): lax.all_to_all(back.reshape(devices, rows, width), 'dev', split_axis=0, c...  3.98 us
    dot_general x1, matrix products, local(): lax.dot_general(select, returned, (((0,), (0,)), ((), ())), preferred_ele...  3.97 us
  transfers between devices with their start and end apart: 2, of which 2 were waited for; matrix products, arithmetic and copies ran while one was open for 8% of the time, Pallas kernels for 0%

profile of v3, /device:TPU:0, one launch (start us, length us, event | category | flops | bytes accessed | tf_op | source)
XLA Modules:
  0.0 133.5 jit_solution(6298088668548847224)
XLA Ops:
  0.6 0.0 copy-start
  0.7 1.4 %select_reduce_fusion.1 = s32[4,512]{1,0:T(4,128)S(1)} fusion(s32[512]{0:T(512)} %param.14, s32[4,512]{1,0:T(4,128)} %bitcast.107), kind=kLoop, calls=%fused_computation.9 | loop fusion | flops 3143680 | bytes 18432 | tf_op jit(solution)/shard_map/reduce_sum | solution.py:20
  2.1 0.9 slice_add_fusion.4
  3.0 2.1 %select_reduce_fusion.6 = (s32[512]{0:T(512)S(1)}, s32[512]{0:T(512)S(1)}, s32[512]{0:T(512)S(1)}, s32[512]{0:T(512)S(1)}, s32[512]{0:T(512)S(1)}, /*index=5*/s32[512]{0:T(512)S(1)}, s32[512]{0:T(512)S(1)}, s32[512]{0:T(512)S(1)}) fusion(s32[512]{0:T(512)S(1)} %bitcast.118, s32[512]{0:T(512)S(1)} %bitcast.119, s32[512]{0:T(512)S(1)} %bitcast.117, ...), kind=kOutput, calls=%fused_computation.56 | convolution fusion | flops 279965696 | bytes 32768 | tf_op jit(solution)/shard_map/dot_general | solution.py:41
  5.0 0.1 stack.34
  5.1 0.1 stack.33
  5.2 0.1 stack.32
  5.3 0.1 stack.31
  5.4 0.1 stack.30
  5.4 0.1 stack.29
  5.5 0.1 stack.28
  5.6 0.1 stack.27
  5.8 0.1 copy.79
  5.9 0.1 copy.80
  6.1 0.2 eq.237
  6.2 3.0 %multiply_convert_fusion = (bf16[512,512]{1,0:T(8,128)(2,1)S(1)}, f32[512,512]{1,0:T(8,128)}) fusion(bf16[512,1024]{1,0:T(8,128)(2,1)S(1)} %copy-done, bf16[1024,512]{1,0:T(8,128)(2,1)} %param.10), kind=kOutput, calls=%fused_computation.73 | convolution fusion | flops 538181632 | bytes 3670016 | tf_op jit(solution)/shard_map/dot_general | solution.py:265
  9.2 0.8 fusion.18
  10.1 0.0 copy-start.19
  10.1 0.0 copy-done.6
  10.1 0.1 copy-done.16
  10.2 2.2 %fusion.5 = bf16[4096,128]{1,0:T(8,128)(2,1)S(1)} fusion(bf16[4096]{0:T(1024)(128)(2,1)S(1)} %eq.237, bf16[512,512]{1,0:T(8,128)(2,1)S(1)} %fusion.18, bf16[512,512]{1,0:T(8,128)(2,1)S(1)} %get-tuple-element.42, bf16[512,128]{1,0:T(8,128)(2,1)S(1)} %copy-done.16), kind=kOutput, calls=%fused_computation.7 | convolution fusion | flops 606666752 | bytes 2236416 | tf_op jit(solution)/shard_map/dot_general | solution.py:268
  12.4 0.0 copy-start.4
  12.4 0.0 copy-start.3
  12.4 1.1 pad_maximum_fusion
  13.5 7.5 %all-to-all-start = ((bf16[32,136,128]{2,1,0:T(8,128)(2,1)}), bf16[32,136,128]{2,1,0:T(8,128)(2,1)S(1)}, u32[]{:S(2)}, u32[]{:S(2)}) async-start(bf16[32,136,128]{2,1,0:T(8,128)(2,1)} %pad_maximum_fusion), calls=%async_computation | async-start | bytes 2228224 | tf_op jit(solution)/shard_map/all_to_all | solution.py:270
  21.0 0.0 copy-done.4
  21.1 5.3 %select_reduce_fusion = f32[16,128]{1,0:T(8,128)S(1)} fusion(f32[16,4096]{1,0:T(8,128)S(1)} %convert_divide_fusion, s32[16,4096]{1,0:T(8,128)S(1)} %copy-done.3), kind=kLoop, calls=%fused_computation | loop fusion | flops 25163776 | bytes 532480 | tf_op jit(solution)/shard_map/reduce_sum | solution.py:59
  26.4 0.2 fusion.55
  26.7 0.1 copy.107
  26.8 21.7 %all-to-all-done = bf16[32,136,128]{2,1,0:T(8,128)(2,1)S(1)} async-done(((bf16[32,136,128]{2,1,0:T(8,128)(2,1)}), bf16[32,136,128]{2,1,0:T(8,128)(2,1)S(1)}, u32[]{:S(2)}, u32[]{:S(2)}) %all-to-all-start) | async-done | bytes 1114144 | tf_op jit(solution)/shard_map/all_to_all | solution.py:270
  48.5 0.1 copy.84
  48.6 0.1 copy.87
  48.7 0.1 copy.88
  48.9 0.0 copy-start.5
  48.9 1.4 %select_reduce_fusion.4 = (f32[16,256]{1,0:T(8,128)S(1)}, f32[16,256]{1,0:T(8,128)S(1)}, f32[16,256]{1,0:T(8,128)S(1)}) fusion(s32[16,256]{1,0:T(8,128)S(1)} %broadcast_add_fusion.1, s32[16,256]{1,0:T(8,128)S(1)} %get-tuple-element.23, s32[16,256]{1,0:T(8,128)S(1)} %get-tuple-element.24, bf16[16,96,128]{2,1,0:T(8,128)(2,1)S(1)} %bitcast.101, ...), kind=kOutput, calls=%fused_computation.30 | convolution fusion | flops 104714240 | bytes 507904 | tf_op jit(solution)/shard_map/cql,chl->cqh/dot_general | solution.py:70
  50.3 0.0 copy-done.1
  50.3 0.0 copy-start.10
  50.3 0.0 copy-done.5
  50.3 1.7 %add_reduce_fusion = (f32[16,256]{1,0:T(8,128)S(1)}, f32[16,256,128]{1,2,0:T(8,128)S(1)}) fusion(f32[16,128]{1,0:T(8,128)S(1)} %log.16, bf16[16,128,128]{2,1,0:T(8,128)(2,1)S(1)} %bitcast.93, bf16[32,136,128]{2,1,0:T(8,128)(2,1)} %copy-done.1), kind=kOutput, calls=%fused_computation.25 | convolution fusion | flops 135262208 | bytes 3694592 | tf_op jit(solution)/shard_map/cqe,cie->cqi/dot_general | solution.py:79
  52.0 1.0 select_reduce_fusion.2
  53.0 0.0 copy-start.12
  53.0 1.3 fusion.52
  54.3 0.0 copy-done.8
  54.3 0.0 copy-done.10
  54.3 1.3 fusion.16
  55.6 1.3 copy.124
  56.9 4.0 %all-to-all-start.1 = ((bf16[32,128,128]{2,1,0:T(8,128)(2,1)}), bf16[32,128,128]{2,1,0:T(8,128)(2,1)}, u32[]{:S(2)}, u32[]{:S(2)}) async-start(bf16[32,128,128]{2,1,0:T(8,128)(2,1)} %bitcast.89), calls=%async_computation.1 | async-start | bytes 2097152 | tf_op jit(solution)/shard_map/all_to_all | solution.py:285
  60.9 0.1 copy.94
  61.0 0.1 copy.95
  61.1 0.1 copy.86
  61.2 0.1 copy.97
  61.3 0.1 copy.93
  61.4 0.1 copy.96
  61.5 0.2 convert_reduce_fusion
  61.7 0.5 div.73
  62.2 2.2 %fusion.23 = f32[16,128,128]{2,1,0:T(8,128)S(1)} fusion(f32[16,256,128]{1,2,0:T(8,128)S(1)} %get-tuple-element.45, f32[16,256]{1,0:T(8,128)} %copy-done.12, s32[16,256]{1,0:T(8,128)} %copy-done.10, f32[16,256]{1,0:T(8,128)S(1)} %get-tuple-element.44, f32[16,128]{1,0:T(8,128)} %copy-done.8, bf16[32,136,128]{2,1,0:T(8,128)(2,1)} %copy-done.1), kind=kOutput, calls=%fused_computation.46 | convolution fusion | flops 138412032 | bytes 4251648 | tf_op jit(solution)/shard_map/cqi,cqe->cie/dot_general | solution.py:99
  64.5 2.0 %convolution_add_fusion = f32[16,128,128]{2,1,0:T(8,128)} fusion(f32[16,128,128]{2,1,0:T(8,128)S(1)} %fusion.23, f32[16,256,128]{1,2,0:T(8,128)S(1)} %get-tuple-element.45, f32[16,256]{1,0:T(8,128)S(1)} %copy-done.13, s32[16,256]{1,0:T(8,128)S(1)} %copy-done.11, f32[16,256]{1,0:T(8,128)S(1)} %get-tuple-element.44, f32[16,128]{1,0:T(8,128)S(1)} %copy-done.9, ...), kind=kOutput, calls=%fused_computation.37 | convolution fusion | flops 139198464 | bytes 5300224 | tf_op jit(solution)/shard_map/cqi,cqe->cie/dot_general | solution.py:101
  66.5 20.3 %all-to-all-done.1 = bf16[32,128,128]{2,1,0:T(8,128)(2,1)} async-done(((bf16[32,128,128]{2,1,0:T(8,128)(2,1)}), bf16[32,128,128]{2,1,0:T(8,128)(2,1)}, u32[]{:S(2)}, u32[]{:S(2)}) %all-to-all-start.1) | async-done | bytes 1048608 | tf_op jit(solution)/shard_map/all_to_all | solution.py:285
  86.8 4.0 %fusion.19 = bf16[512,128]{1,0:T(8,128)(2,1)S(1)} fusion(bf16[4096,128]{1,0:T(8,128)(2,1)} %bitcast.33, bf16[512,512]{1,0:T(8,128)(2,1)} %copy-done.19, bf16[8]{0:T(256)(128)(2,1)S(1)} %copy-done.15), kind=kOutput, calls=%fused_computation.42 | convolution fusion | flops 539033600 | bytes 1703952 | tf_op jit(solution)/shard_map/dot_general | solution.py:288
  90.8 1.0 fusion.73.small_ref
  91.9 2.3 %convolution_bitcast_fusion.big_ref = f32[1024,512]{1,0:T(8,128)} fusion(bf16[512,1024]{1,0:T(8,128)(2,1)S(1)} %copy-done, bf16[512,128]{1,0:T(8,128)(2,1)S(1)} %fusion.19, bf16[512,128]{1,0:T(8,128)(2,1)S(1)} %copy-done.17, f32[512,512]{1,0:T(8,128)S(1)} %copy-done.18), kind=kOutput, calls=%fused_computation.27 | convolution fusion | flops 606339072 | bytes 4456448 | tf_op jit(solution)/shard_map/dot_general | solution.py:294
  94.2 34.9 %sum_over_devices.1 = (bf16[1024,512]{1,0:T(8,128)(2,1)}, bf16[512,128]{1,0:T(8,128)(2,1)}) custom-call(f32[1024,512]{1,0:T(8,128)} %convolution_bitcast_fusion.big_ref, f32[512,128]{1,0:T(8,128)} %fusion.73.small_ref), custom_call_target="tpu_custom_call" | custom-call | tf_op jit(solution)/shard_map/sum_over_devices/pallas_call | solution.py:222
  129.1 1.6 %convert_element_type.95 = f32[512,128]{1,0:T(8,128)} convert(bf16[512,128]{1,0:T(8,128)(2,1)} %get-tuple-element.7) | non-fusion elementwise | flops 65536 | bytes 393216 | tf_op jit(solution)/shard_map/convert_element_type | solution.py:241
  130.7 2.8 %convert_element_type.94 = f32[1024,512]{1,0:T(8,128)} convert(bf16[1024,512]{1,0:T(8,128)(2,1)} %get-tuple-element.6) | non-fusion elementwise | flops 524288 | bytes 3145728 | tf_op jit(solution)/shard_map/convert_element_type | solution.py:241
  (53 shorter events, 0.4 us)
Async XLA Ops:
  0.6 5.6 %copy-start = (bf16[512,1024]{1,0:T(8,128)(2,1)S(1)}, bf16[512,1024]{1,0:T(8,128)(2,1)}, u32[]{:S(2)}) copy-start(bf16[512,1024]{1,0:T(8,128)(2,1)} %param.9) | copy-start | bytes 3145732
  0.7 5.4 %copy-start.14 = (bf16[8]{0:T(256)(128)(2,1)}, bf16[8]{0:T(256)(128)(2,1)S(1)}, u32[]{:S(2)}) copy-start(bf16[8]{0:T(256)(128)(2,1)S(1)} %iota_convert_fusion) | copy-start | bytes 52
  9.2 0.9 copy-start.6
  9.2 1.0 copy-start.16
  10.1 2.3 %copy-start.19 = (bf16[512,512]{1,0:T(8,128)(2,1)}, bf16[512,512]{1,0:T(8,128)(2,1)S(1)}, u32[]{:S(2)}) copy-start(bf16[512,512]{1,0:T(8,128)(2,1)S(1)} %fusion.18) | copy-start | bytes 1572868
  12.4 8.6 %copy-start.4 = (s32[16,4096]{1,0:T(8,128)S(1)}, s32[16,4096]{1,0:T(8,128)}, u32[]{:S(2)}) copy-start(s32[16,4096]{1,0:T(8,128)} %param.16) | copy-start | bytes 786436
  12.4 8.7 %copy-start.3 = (s32[16,4096]{1,0:T(8,128)S(1)}, s32[16,4096]{1,0:T(8,128)}, u32[]{:S(2)}) copy-start(s32[16,4096]{1,0:T(8,128)} %param.15) | copy-start | bytes 786436
  13.5 34.9 %all-to-all-start = ((bf16[32,136,128]{2,1,0:T(8,128)(2,1)}), bf16[32,136,128]{2,1,0:T(8,128)(2,1)S(1)}, u32[]{:S(2)}, u32[]{:S(2)}) async-start(bf16[32,136,128]{2,1,0:T(8,128)(2,1)} %pad_maximum_fusion), calls=%async_computation | async-start | bytes 2228224 | tf_op jit(solution)/shard_map/all_to_all | solution.py:270
  26.4 27.9 %copy-start.8 = (f32[16,128]{1,0:T(8,128)}, f32[16,128]{1,0:T(8,128)S(1)}, u32[]{:S(2)}) copy-start(f32[16,128]{1,0:T(8,128)S(1)} %log.16) | copy-start | bytes 24580
  48.5 1.8 %copy-start.1 = (bf16[32,136,128]{2,1,0:T(8,128)(2,1)}, bf16[32,136,128]{2,1,0:T(8,128)(2,1)S(1)}, u32[]{:S(2)}) copy-start(bf16[32,136,128]{2,1,0:T(8,128)(2,1)S(1)} %all-to-all-done) | copy-start | bytes 3342340
  48.9 1.5 %copy-start.5 = (bf16[2048,128]{1,0:T(8,128)(2,1)S(1)}, bf16[2048,128]{1,0:T(8,128)(2,1)}, u32[]{:S(2)}) copy-start(bf16[2048,128]{1,0:T(8,128)(2,1)} %param.12) | copy-start | bytes 1572868
  50.3 4.0 %copy-start.10 = (s32[16,256]{1,0:T(8,128)}, s32[16,256]{1,0:T(8,128)S(1)}, u32[]{:S(2)}) copy-start(s32[16,256]{1,0:T(8,128)S(1)} %convert_select_fusion) | copy-start | bytes 49156
  53.0 8.1 %copy-start.12 = (f32[16,256]{1,0:T(8,128)}, f32[16,256]{1,0:T(8,128)S(1)}, u32[]{:S(2)}) copy-start(f32[16,256]{1,0:T(8,128)S(1)} %get-tuple-element.9) | copy-start | bytes 49156
  56.9 29.9 %all-to-all-start.1 = ((bf16[32,128,128]{2,1,0:T(8,128)(2,1)}), bf16[32,128,128]{2,1,0:T(8,128)(2,1)}, u32[]{:S(2)}, u32[]{:S(2)}) async-start(bf16[32,128,128]{2,1,0:T(8,128)(2,1)} %bitcast.89), calls=%async_computation.1 | async-start | bytes 2097152 | tf_op jit(solution)/shard_map/all_to_all | solution.py:285
  62.2 2.2 %copy-start.2 = (bf16[32,136,128]{2,1,0:T(8,128)(2,1)S(1)}, bf16[32,136,128]{2,1,0:T(8,128)(2,1)}, u32[]{:S(2)}) copy-start(bf16[32,136,128]{2,1,0:T(8,128)(2,1)} %copy-done.1) | copy-start | bytes 3342340
  62.2 2.3 %copy-start.9 = (f32[16,128]{1,0:T(8,128)S(1)}, f32[16,128]{1,0:T(8,128)}, u32[]{:S(2)}) copy-start(f32[16,128]{1,0:T(8,128)} %copy-done.8) | copy-start | bytes 24580
  62.2 2.3 %copy-start.11 = (s32[16,256]{1,0:T(8,128)S(1)}, s32[16,256]{1,0:T(8,128)}, u32[]{:S(2)}) copy-start(s32[16,256]{1,0:T(8,128)} %copy-done.10) | copy-start | bytes 49156
  62.2 2.3 %copy-start.13 = (f32[16,256]{1,0:T(8,128)S(1)}, f32[16,256]{1,0:T(8,128)}, u32[]{:S(2)}) copy-start(f32[16,256]{1,0:T(8,128)} %copy-done.12) | copy-start | bytes 49156
  64.5 22.3 %copy-start.15 = (bf16[8]{0:T(256)(128)(2,1)S(1)}, bf16[8]{0:T(256)(128)(2,1)}, u32[]{:S(2)}) copy-start(bf16[8]{0:T(256)(128)(2,1)} %copy-done.14) | copy-start | bytes 52
  86.8 4.0 %copy-start.7 = (bf16[512,512]{1,0:T(8,128)(2,1)S(1)}, bf16[512,512]{1,0:T(8,128)(2,1)}, u32[]{:S(2)}) copy-start(bf16[512,512]{1,0:T(8,128)(2,1)} %copy-done.6) | copy-start | bytes 1572868
  86.8 5.0 %copy-start.17 = (bf16[512,128]{1,0:T(8,128)(2,1)S(1)}, bf16[512,128]{1,0:T(8,128)(2,1)}, u32[]{:S(2)}) copy-start(bf16[512,128]{1,0:T(8,128)(2,1)} %param.11) | copy-start | bytes 393220
  86.8 5.0 %copy-start.18 = (f32[512,512]{1,0:T(8,128)S(1)}, f32[512,512]{1,0:T(8,128)}, u32[]{:S(2)}) copy-start(f32[512,512]{1,0:T(8,128)} %get-tuple-element.43) | copy-start | bytes 3145732

commit v4 on v3

--- a/solution.py
+++ b/solution.py
@@ -105,17 +105,23 @@
     return cluster_loss, dquery, dtable
 
 
-LANES = 3
-
-
-def bit_orders(bits):
+ORDERS = 3
+TILE = 16
+
+
+def row_groups(bits, tiles):
     turn = [b for b in (1, 2, 3) if b < bits]
     rest = [b for b in range(bits) if b > 3]
-    orders = []
-    for lane in range(LANES):
-        k = lane % max(1, len(turn))
-        orders.append([0] + turn[k:] + turn[:k] + rest)
-    return orders
+    shares = [tiles] if tiles == 1 else [tiles - tiles // 2, tiles // 2]
+    groups = []
+    start = 0
+    for share in shares:
+        for k in range(ORDERS):
+            k = k % max(1, len(turn))
+            size = (share * TILE) << bits
+            groups.append((start, size, [0] + turn[k:] + turn[:k] + rest))
+            start += size
+    return groups
 
 
 def blocks_of(ref):
@@ -123,13 +129,13 @@
     return [(c, rows) for c in range(columns // 128)]
 
 
-def reduce_kernel(bits, unit, big_ref, small_ref, big_out, small_out, acc, out, inbox, full, send, recv):
+def reduce_kernel(bits, tiles, big_ref, small_ref, big_out, small_out, acc, out, inbox, full, send, recv):
     me = lax.axis_index("dev")
     mesh = pl.DeviceIdType.MESH
-    orders = bit_orders(bits)
-    per_lane = unit << bits
-    partners = [me + (1 << b) * (1 - 2 * ((me // (1 << b)) % 2)) for b in range(bits)]
+    groups = row_groups(bits, tiles)
+    total = groups[-1][0] + groups[-1][1]
     bit = [(me // (1 << b)) % 2 for b in range(bits)]
+    partners = [me + (1 << b) * (1 - 2 * bit[b]) for b in range(bits)]
 
     barrier = pltpu.get_barrier_semaphore()
     for b in range(bits):
@@ -139,71 +145,74 @@
         for c, rows in blocks_of(ref):
             acc[row : row + rows, :] = ref[:, c * 128 : (c + 1) * 128]
             row += rows
-    if row < LANES * per_lane:
-        acc[row:, :] = jnp.zeros((LANES * per_lane - row, 128), jnp.float32)
-
-    off = [lane * per_lane for lane in range(LANES)]
-    length = per_lane
-    gap = []
-    at = 0
+    if row < total:
+        acc[row:, :] = jnp.zeros((total - row, 128), jnp.float32)
+
+    def rows_at(first, count):
+        return pl.ds(pl.multiple_of(first, TILE), count)
+
+    off = [start for start, _, _ in groups]
+    length = [size for _, size, _ in groups]
+    waiting = [None] * len(groups)
+    landed = [0] * len(groups)
+    started = []
+
+    def take(g):
+        waiting[g].wait_recv()
+        kept = rows_at(off[g], length[g])
+        got = inbox[pl.ds(groups[g][0] + landed[g], length[g]), :].astype(jnp.float32)
+        acc[kept, :] = acc[kept, :] + got
+        landed[g] += length[g]
+
     for s in range(bits):
-        gap.append(at)
-        at += per_lane >> (s + 1)
-    started = []
-
-    def rows_at(first, count):
-        return pl.ds(pl.multiple_of(first, 16), count)
-
-    for s in range(bits):
-        half = length // 2
-        copies = []
-        for lane in range(LANES):
-            b = orders[lane][s]
-            give = off[lane] + (1 - bit[b]) * half
-            off[lane] = off[lane] + bit[b] * half
+        for g in range(len(groups)):
+            start, _, order = groups[g]
+            if s > 0:
+                take(g)
+            b = order[s]
+            half = length[g] // 2
+            give = off[g] + (1 - bit[b]) * half
+            off[g] = off[g] + bit[b] * half
+            length[g] = half
             out[rows_at(give, half), :] = acc[rows_at(give, half), :].astype(jnp.bfloat16)
-            if s == 0 and lane == 0:
+            if s == 0 and g == 0:
                 pl.semaphore_wait(barrier, bits)
             copy = pltpu.make_async_remote_copy(
                 src_ref=out.at[rows_at(give, half), :],
-                dst_ref=inbox.at[pl.ds(lane * per_lane + gap[s], half), :],
-                send_sem=send.at[lane, s],
-                recv_sem=recv.at[lane, s],
+                dst_ref=inbox.at[pl.ds(start + landed[g], half), :],
+                send_sem=send.at[g, s],
+                recv_sem=recv.at[g, s],
                 device_id=(partners[b],),
                 device_id_type=mesh,
             )
             copy.start()
-            copies.append(copy)
+            waiting[g] = copy
             started.append(copy)
-        for lane in range(LANES):
-            copies[lane].wait_recv()
-            kept = rows_at(off[lane], half)
-            got = inbox[pl.ds(lane * per_lane + gap[s], half), :].astype(jnp.float32)
-            acc[kept, :] = acc[kept, :] + got
-        length = half
-    for lane in range(LANES):
-        kept = rows_at(off[lane], length)
-        full[kept, :] = acc[kept, :].astype(jnp.bfloat16)
     for s in range(bits - 1, -1, -1):
-        copies = []
-        for lane in range(LANES):
-            b = orders[lane][s]
-            held = rows_at(off[lane], length)
+        for g in range(len(groups)):
+            if s == bits - 1:
+                take(g)
+                kept = rows_at(off[g], length[g])
+                full[kept, :] = acc[kept, :].astype(jnp.bfloat16)
+            else:
+                waiting[g].wait_recv()
+            b = groups[g][2][s]
+            held = rows_at(off[g], length[g])
             copy = pltpu.make_async_remote_copy(
                 src_ref=full.at[held, :],
                 dst_ref=full.at[held, :],
-                send_sem=send.at[lane, bits + s],
-                recv_sem=recv.at[lane, bits + s],
+                send_sem=send.at[g, bits + s],
+                recv_sem=recv.at[g, bits + s],
                 device_id=(partners[b],),
                 device_id_type=mesh,
             )
             copy.start()
-            copies.append(copy)
+            waiting[g] = copy
             started.append(copy)
-            off[lane] = off[lane] - bit[b] * length
-        for lane in range(LANES):
-            copies[lane].wait_recv()
-        length = length * 2
+            off[g] = off[g] - bit[b] * length[g]
+            length[g] = length[g] * 2
+    for copy in waiting:
+        copy.wait_recv()
     for copy in started:
         copy.wait_send()
     row = 0
@@ -216,11 +225,11 @@
 def sum_over_devices(big, small):
     devices = lax.axis_size("dev")
     bits = devices.bit_length() - 1
-    total = (big.size + small.size) // 128
-    unit = -(-total // (LANES * devices * 16)) * 16
-    rows = LANES * devices * unit
+    tiles = -(-((big.size + small.size) // 128) // (ORDERS * devices * TILE))
+    groups = row_groups(bits, tiles)
+    rows = groups[-1][0] + groups[-1][1]
     summed = pl.pallas_call(
-        functools.partial(reduce_kernel, bits, unit),
+        functools.partial(reduce_kernel, bits, tiles),
         out_shape=(
             jax.ShapeDtypeStruct(big.shape, jnp.bfloat16),
             jax.ShapeDtypeStruct(small.shape, jnp.bfloat16),
@@ -232,8 +241,8 @@
             pltpu.VMEM((rows, 128), jnp.bfloat16),
             pltpu.VMEM((rows, 128), jnp.bfloat16),
             pltpu.VMEM((rows, 128), jnp.bfloat16),
-            pltpu.SemaphoreType.DMA((LANES, 2 * bits)),
-            pltpu.SemaphoreType.DMA((LANES, 2 * bits)),
+            pltpu.SemaphoreType.DMA((len(groups), 2 * bits)),
+            pltpu.SemaphoreType.DMA((len(groups), 2 * bits)),
         ],
         compiler_params=pltpu.CompilerParams(collective_id=0, has_side_effects=True),
         name="sum_over_devices",

time: 134 us -> 132 us (0.985)
  Pallas kernels: 34.9 us -> 32.8 us
    pallas_call x1, Pallas kernels: 34.9 us -> 32.8 us  [sum_over_devices(): pl.pallas_call(functools.partial(reduce_kernel, bits, tiles), out_shape=(...]
  transfers between devices with their start and end apart: 2 -> 2, of which waited for: 2 -> 2; matrix products, arithmetic and copies ran while one was open for 8% -> 9% of each run, Pallas kernels for 0% -> 0%
where the time goes in v4:
time: 132 us; the launch traced here: 131 us
  waiting for transfers between devices  42 us (32%)
  Pallas kernels  32.8 us (25%)
  matrix products  25.3 us (19%)
  other arithmetic  15.2 us (12%)
  starting transfers between devices  11.5 us (9%)
  local copies, waits for them, and re-layouts  3.48 us (3%)
    pallas_call x1, Pallas kernels, sum_over_devices(): pl.pallas_call(functools.partial(reduce_kernel, bits, tiles), out_shape=(...  32.8 us
    all_to_all x1, waiting for transfers between devices, local(): lax.all_to_all(payload, 'dev', split_axis=0, concat_axis=0, tiled=True)  21.7 us
    all_to_all x1, waiting for transfers between devices, local(): lax.all_to_all(back.reshape(devices, rows, width), 'dev', split_axis=0, c...  20.3 us
    all_to_all x1, starting transfers between devices, local(): lax.all_to_all(payload, 'dev', split_axis=0, concat_axis=0, tiled=True)  7.51 us
    reduce_sum x1, other arithmetic, owner(): jnp.sum(jnp.where(table_ids[:, None, :] == which, recip[:, None, :], 0.0)...  5.26 us
    convert_element_type x2, other arithmetic, sum_over_devices(): return tuple((part.astype(jnp.float32) for part in summed))  4.46 us
    all_to_all x1, starting transfers between devices, local(): lax.all_to_all(back.reshape(devices, rows, width), 'dev', split_axis=0, c...  3.98 us
    dot_general x1, matrix products, local(): lax.dot_general(select, returned, (((0,), (0,)), ((), ())), preferred_ele...  3.97 us
  transfers between devices with their start and end apart: 2, of which 2 were waited for; matrix products, arithmetic and copies ran while one was open for 9% of the time, Pallas kernels for 0%

profile of v4, /device:TPU:0, one launch (start us, length us, event | category | flops | bytes accessed | tf_op | source)
XLA Modules:
  0.0 131.4 jit_solution(2711218741130461113)
XLA Ops:
  0.6 0.0 copy-start
  0.7 0.0 copy-start.14
  0.7 1.4 %select_reduce_fusion.1 = s32[4,512]{1,0:T(4,128)S(1)} fusion(s32[512]{0:T(512)} %param.14, s32[4,512]{1,0:T(4,128)} %bitcast.107), kind=kLoop, calls=%fused_computation.9 | loop fusion | flops 3143680 | bytes 18432 | tf_op jit(solution)/shard_map/reduce_sum | solution.py:20
  2.1 0.9 slice_add_fusion.4
  3.0 2.1 %select_reduce_fusion.6 = (s32[512]{0:T(512)S(1)}, s32[512]{0:T(512)S(1)}, s32[512]{0:T(512)S(1)}, s32[512]{0:T(512)S(1)}, s32[512]{0:T(512)S(1)}, /*index=5*/s32[512]{0:T(512)S(1)}, s32[512]{0:T(512)S(1)}, s32[512]{0:T(512)S(1)}) fusion(s32[512]{0:T(512)S(1)} %bitcast.118, s32[512]{0:T(512)S(1)} %bitcast.119, s32[512]{0:T(512)S(1)} %bitcast.117, ...), kind=kOutput, calls=%fused_computation.56 | convolution fusion | flops 279965696 | bytes 32768 | tf_op jit(solution)/shard_map/dot_general | solution.py:41
  5.0 0.1 stack.34
  5.1 0.1 stack.33
  5.2 0.1 stack.32
  5.3 0.1 stack.31
  5.4 0.1 stack.30
  5.4 0.1 stack.29
  5.5 0.1 stack.28
  5.6 0.1 stack.27
  5.8 0.1 copy.79
  5.9 0.1 copy.80
  6.0 0.0 copy-done.14
  6.1 0.2 eq.237
  6.2 0.0 copy-done
  6.2 3.0 %multiply_convert_fusion = (bf16[512,512]{1,0:T(8,128)(2,1)S(1)}, f32[512,512]{1,0:T(8,128)}) fusion(bf16[512,1024]{1,0:T(8,128)(2,1)S(1)} %copy-done, bf16[1024,512]{1,0:T(8,128)(2,1)} %param.10), kind=kOutput, calls=%fused_computation.73 | convolution fusion | flops 538181632 | bytes 3670016 | tf_op jit(solution)/shard_map/dot_general | solution.py:274
  9.2 0.8 fusion.18
  10.1 0.0 copy-start.19
  10.1 0.1 copy-done.16
  10.2 2.2 %fusion.5 = bf16[4096,128]{1,0:T(8,128)(2,1)S(1)} fusion(bf16[4096]{0:T(1024)(128)(2,1)S(1)} %eq.237, bf16[512,512]{1,0:T(8,128)(2,1)S(1)} %fusion.18, bf16[512,512]{1,0:T(8,128)(2,1)S(1)} %get-tuple-element.42, bf16[512,128]{1,0:T(8,128)(2,1)S(1)} %copy-done.16), kind=kOutput, calls=%fused_computation.7 | convolution fusion | flops 606666752 | bytes 2236416 | tf_op jit(solution)/shard_map/dot_general | solution.py:277
  12.4 0.0 copy-done.19
  12.4 0.0 copy-start.4
  12.4 0.0 copy-start.3
  12.4 1.1 pad_maximum_fusion
  13.5 7.5 %all-to-all-start = ((bf16[32,136,128]{2,1,0:T(8,128)(2,1)}), bf16[32,136,128]{2,1,0:T(8,128)(2,1)S(1)}, u32[]{:S(2)}, u32[]{:S(2)}) async-start(bf16[32,136,128]{2,1,0:T(8,128)(2,1)} %pad_maximum_fusion), calls=%async_computation | async-start | bytes 2228224 | tf_op jit(solution)/shard_map/all_to_all | solution.py:279
  21.1 5.3 %select_reduce_fusion = f32[16,128]{1,0:T(8,128)S(1)} fusion(f32[16,4096]{1,0:T(8,128)S(1)} %convert_divide_fusion, s32[16,4096]{1,0:T(8,128)S(1)} %copy-done.3), kind=kLoop, calls=%fused_computation | loop fusion | flops 25163776 | bytes 532480 | tf_op jit(solution)/shard_map/reduce_sum | solution.py:59
  26.4 0.2 fusion.55
  26.7 0.1 copy.107
  26.8 21.7 %all-to-all-done = bf16[32,136,128]{2,1,0:T(8,128)(2,1)S(1)} async-done(((bf16[32,136,128]{2,1,0:T(8,128)(2,1)}), bf16[32,136,128]{2,1,0:T(8,128)(2,1)S(1)}, u32[]{:S(2)}, u32[]{:S(2)}) %all-to-all-start) | async-done | bytes 1114144 | tf_op jit(solution)/shard_map/all_to_all | solution.py:279
  48.5 0.1 copy.84
  48.6 0.1 copy.87
  48.7 0.1 copy.88
  48.9 0.0 copy-start.5
  48.9 1.4 %select_reduce_fusion.4 = (f32[16,256]{1,0:T(8,128)S(1)}, f32[16,256]{1,0:T(8,128)S(1)}, f32[16,256]{1,0:T(8,128)S(1)}) fusion(s32[16,256]{1,0:T(8,128)S(1)} %broadcast_add_fusion.1, s32[16,256]{1,0:T(8,128)S(1)} %get-tuple-element.23, s32[16,256]{1,0:T(8,128)S(1)} %get-tuple-element.24, bf16[16,96,128]{2,1,0:T(8,128)(2,1)S(1)} %bitcast.101, ...), kind=kOutput, calls=%fused_computation.30 | convolution fusion | flops 104714240 | bytes 507904 | tf_op jit(solution)/shard_map/cql,chl->cqh/dot_general | solution.py:70
  50.3 0.0 copy-start.10
  50.3 1.7 %add_reduce_fusion = (f32[16,256]{1,0:T(8,128)S(1)}, f32[16,256,128]{1,2,0:T(8,128)S(1)}) fusion(f32[16,128]{1,0:T(8,128)S(1)} %log.16, bf16[16,128,128]{2,1,0:T(8,128)(2,1)S(1)} %bitcast.93, bf16[32,136,128]{2,1,0:T(8,128)(2,1)} %copy-done.1), kind=kOutput, calls=%fused_computation.25 | convolution fusion | flops 135262208 | bytes 3694592 | tf_op jit(solution)/shard_map/cqe,cie->cqi/dot_general | solution.py:79
  52.0 1.0 select_reduce_fusion.2
  53.0 0.0 copy-start.12
  53.0 1.3 fusion.52
  54.3 1.3 fusion.16
  55.6 1.3 copy.124
  56.9 4.0 %all-to-all-start.1 = ((bf16[32,128,128]{2,1,0:T(8,128)(2,1)}), bf16[32,128,128]{2,1,0:T(8,128)(2,1)}, u32[]{:S(2)}, u32[]{:S(2)}) async-start(bf16[32,128,128]{2,1,0:T(8,128)(2,1)} %bitcast.89), calls=%async_computation.1 | async-start | bytes 2097152 | tf_op jit(solution)/shard_map/all_to_all | solution.py:294
  60.9 0.1 copy.94
  61.0 0.1 copy.95
  61.1 0.1 copy.86
  61.2 0.1 copy.97
  61.3 0.1 copy.93
  61.4 0.1 copy.96
  61.5 0.2 convert_reduce_fusion
  61.7 0.5 div.73
  62.2 2.2 %fusion.23 = f32[16,128,128]{2,1,0:T(8,128)S(1)} fusion(f32[16,256,128]{1,2,0:T(8,128)S(1)} %get-tuple-element.45, f32[16,256]{1,0:T(8,128)} %copy-done.12, s32[16,256]{1,0:T(8,128)} %copy-done.10, f32[16,256]{1,0:T(8,128)S(1)} %get-tuple-element.44, f32[16,128]{1,0:T(8,128)} %copy-done.8, bf16[32,136,128]{2,1,0:T(8,128)(2,1)} %copy-done.1), kind=kOutput, calls=%fused_computation.46 | convolution fusion | flops 138412032 | bytes 4251648 | tf_op jit(solution)/shard_map/cqi,cqe->cie/dot_general | solution.py:99
  64.5 2.0 %convolution_add_fusion = f32[16,128,128]{2,1,0:T(8,128)} fusion(f32[16,128,128]{2,1,0:T(8,128)S(1)} %fusion.23, f32[16,256,128]{1,2,0:T(8,128)S(1)} %get-tuple-element.45, f32[16,256]{1,0:T(8,128)S(1)} %copy-done.13, s32[16,256]{1,0:T(8,128)S(1)} %copy-done.11, f32[16,256]{1,0:T(8,128)S(1)} %get-tuple-element.44, f32[16,128]{1,0:T(8,128)S(1)} %copy-done.9, ...), kind=kOutput, calls=%fused_computation.37 | convolution fusion | flops 139198464 | bytes 5300224 | tf_op jit(solution)/shard_map/cqi,cqe->cie/dot_general | solution.py:101
  66.5 20.3 %all-to-all-done.1 = bf16[32,128,128]{2,1,0:T(8,128)(2,1)} async-done(((bf16[32,128,128]{2,1,0:T(8,128)(2,1)}), bf16[32,128,128]{2,1,0:T(8,128)(2,1)}, u32[]{:S(2)}, u32[]{:S(2)}) %all-to-all-start.1) | async-done | bytes 1048608 | tf_op jit(solution)/shard_map/all_to_all | solution.py:294
  86.8 0.0 copy-done.15
  86.8 4.0 %fusion.19 = bf16[512,128]{1,0:T(8,128)(2,1)S(1)} fusion(bf16[4096,128]{1,0:T(8,128)(2,1)} %bitcast.33, bf16[512,512]{1,0:T(8,128)(2,1)} %copy-done.19, bf16[8]{0:T(256)(128)(2,1)S(1)} %copy-done.15), kind=kOutput, calls=%fused_computation.42 | convolution fusion | flops 539033600 | bytes 1703952 | tf_op jit(solution)/shard_map/dot_general | solution.py:297
  90.8 1.0 fusion.73.small_ref
  91.8 0.0 copy-done.18
  91.9 2.3 %convolution_bitcast_fusion.big_ref = f32[1024,512]{1,0:T(8,128)} fusion(bf16[512,1024]{1,0:T(8,128)(2,1)S(1)} %copy-done, bf16[512,128]{1,0:T(8,128)(2,1)S(1)} %fusion.19, bf16[512,128]{1,0:T(8,128)(2,1)S(1)} %copy-done.17, f32[512,512]{1,0:T(8,128)S(1)} %copy-done.18), kind=kOutput, calls=%fused_computation.27 | convolution fusion | flops 606339072 | bytes 4456448 | tf_op jit(solution)/shard_map/dot_general | solution.py:303
  94.2 32.8 %sum_over_devices.1 = (bf16[1024,512]{1,0:T(8,128)(2,1)}, bf16[512,128]{1,0:T(8,128)(2,1)}) custom-call(f32[1024,512]{1,0:T(8,128)} %convolution_bitcast_fusion.big_ref, f32[512,128]{1,0:T(8,128)} %fusion.73.small_ref), custom_call_target="tpu_custom_call" | custom-call | tf_op jit(solution)/shard_map/sum_over_devices/pallas_call | solution.py:231
  127.0 1.6 %convert_element_type.95 = f32[512,128]{1,0:T(8,128)} convert(bf16[512,128]{1,0:T(8,128)(2,1)} %get-tuple-element.7) | non-fusion elementwise | flops 65536 | bytes 393216 | tf_op jit(solution)/shard_map/convert_element_type | solution.py:250
  128.6 2.8 %convert_element_type.94 = f32[1024,512]{1,0:T(8,128)} convert(bf16[1024,512]{1,0:T(8,128)(2,1)} %get-tuple-element.6) | non-fusion elementwise | flops 524288 | bytes 3145728 | tf_op jit(solution)/shard_map/convert_element_type | solution.py:250
  (53 shorter events, 0.4 us)
Async XLA Ops:
  0.6 5.6 %copy-start = (bf16[512,1024]{1,0:T(8,128)(2,1)S(1)}, bf16[512,1024]{1,0:T(8,128)(2,1)}, u32[]{:S(2)}) copy-start(bf16[512,1024]{1,0:T(8,128)(2,1)} %param.9) | copy-start | bytes 3145732
  0.7 5.4 %copy-start.14 = (bf16[8]{0:T(256)(128)(2,1)}, bf16[8]{0:T(256)(128)(2,1)S(1)}, u32[]{:S(2)}) copy-start(bf16[8]{0:T(256)(128)(2,1)S(1)} %iota_convert_fusion) | copy-start | bytes 52
  9.2 0.9 copy-start.6
  9.2 1.0 copy-start.16
  10.1 2.3 %copy-start.19 = (bf16[512,512]{1,0:T(8,128)(2,1)}, bf16[512,512]{1,0:T(8,128)(2,1)S(1)}, u32[]{:S(2)}) copy-start(bf16[512,512]{1,0:T(8,128)(2,1)S(1)} %fusion.18) | copy-start | bytes 1572868
  12.4 8.6 %copy-start.4 = (s32[16,4096]{1,0:T(8,128)S(1)}, s32[16,4096]{1,0:T(8,128)}, u32[]{:S(2)}) copy-start(s32[16,4096]{1,0:T(8,128)} %param.16) | copy-start | bytes 786436
  12.4 8.7 %copy-start.3 = (s32[16,4096]{1,0:T(8,128)S(1)}, s32[16,4096]{1,0:T(8,128)}, u32[]{:S(2)}) copy-start(s32[16,4096]{1,0:T(8,128)} %param.15) | copy-start | bytes 786436
  13.5 34.9 %all-to-all-start = ((bf16[32,136,128]{2,1,0:T(8,128)(2,1)}), bf16[32,136,128]{2,1,0:T(8,128)(2,1)S(1)}, u32[]{:S(2)}, u32[]{:S(2)}) async-start(bf16[32,136,128]{2,1,0:T(8,128)(2,1)} %pad_maximum_fusion), calls=%async_computation | async-start | bytes 2228224 | tf_op jit(solution)/shard_map/all_to_all | solution.py:279
  26.4 27.9 %copy-start.8 = (f32[16,128]{1,0:T(8,128)}, f32[16,128]{1,0:T(8,128)S(1)}, u32[]{:S(2)}) copy-start(f32[16,128]{1,0:T(8,128)S(1)} %log.16) | copy-start | bytes 24580
  48.5 1.8 %copy-start.1 = (bf16[32,136,128]{2,1,0:T(8,128)(2,1)}, bf16[32,136,128]{2,1,0:T(8,128)(2,1)S(1)}, u32[]{:S(2)}) copy-start(bf16[32,136,128]{2,1,0:T(8,128)(2,1)S(1)} %all-to-all-done) | copy-start | bytes 3342340
  48.9 1.5 %copy-start.5 = (bf16[2048,128]{1,0:T(8,128)(2,1)S(1)}, bf16[2048,128]{1,0:T(8,128)(2,1)}, u32[]{:S(2)}) copy-start(bf16[2048,128]{1,0:T(8,128)(2,1)} %param.12) | copy-start | bytes 1572868
  50.3 4.0 %copy-start.10 = (s32[16,256]{1,0:T(8,128)}, s32[16,256]{1,0:T(8,128)S(1)}, u32[]{:S(2)}) copy-start(s32[16,256]{1,0:T(8,128)S(1)} %convert_select_fusion) | copy-start | bytes 49156
  53.0 8.1 %copy-start.12 = (f32[16,256]{1,0:T(8,128)}, f32[16,256]{1,0:T(8,128)S(1)}, u32[]{:S(2)}) copy-start(f32[16,256]{1,0:T(8,128)S(1)} %get-tuple-element.9) | copy-start | bytes 49156
  56.9 29.9 %all-to-all-start.1 = ((bf16[32,128,128]{2,1,0:T(8,128)(2,1)}), bf16[32,128,128]{2,1,0:T(8,128)(2,1)}, u32[]{:S(2)}, u32[]{:S(2)}) async-start(bf16[32,128,128]{2,1,0:T(8,128)(2,1)} %bitcast.89), calls=%async_computation.1 | async-start | bytes 2097152 | tf_op jit(solution)/shard_map/all_to_all | solution.py:294
  62.2 2.2 %copy-start.2 = (bf16[32,136,128]{2,1,0:T(8,128)(2,1)S(1)}, bf16[32,136,128]{2,1,0:T(8,128)(2,1)}, u32[]{:S(2)}) copy-start(bf16[32,136,128]{2,1,0:T(8,128)(2,1)} %copy-done.1) | copy-start | bytes 3342340
  62.2 2.3 %copy-start.9 = (f32[16,128]{1,0:T(8,128)S(1)}, f32[16,128]{1,0:T(8,128)}, u32[]{:S(2)}) copy-start(f32[16,128]{1,0:T(8,128)} %copy-done.8) | copy-start | bytes 24580
  62.2 2.3 %copy-start.11 = (s32[16,256]{1,0:T(8,128)S(1)}, s32[16,256]{1,0:T(8,128)}, u32[]{:S(2)}) copy-start(s32[16,256]{1,0:T(8,128)} %copy-done.10) | copy-start | bytes 49156
  62.2 2.3 %copy-start.13 = (f32[16,256]{1,0:T(8,128)S(1)}, f32[16,256]{1,0:T(8,128)}, u32[]{:S(2)}) copy-start(f32[16,256]{1,0:T(8,128)} %copy-done.12) | copy-start | bytes 49156
  64.5 22.3 %copy-start.15 = (bf16[8]{0:T(256)(128)(2,1)S(1)}, bf16[8]{0:T(256)(128)(2,1)}, u32[]{:S(2)}) copy-start(bf16[8]{0:T(256)(128)(2,1)} %copy-done.14) | copy-start | bytes 52
  86.8 4.0 %copy-start.7 = (bf16[512,512]{1,0:T(8,128)(2,1)S(1)}, bf16[512,512]{1,0:T(8,128)(2,1)}, u32[]{:S(2)}) copy-start(bf16[512,512]{1,0:T(8,128)(2,1)} %copy-done.6) | copy-start | bytes 1572868
  86.8 5.0 %copy-start.17 = (bf16[512,128]{1,0:T(8,128)(2,1)S(1)}, bf16[512,128]{1,0:T(8,128)(2,1)}, u32[]{:S(2)}) copy-start(bf16[512,128]{1,0:T(8,128)(2,1)} %param.11) | copy-start | bytes 393220
  86.8 5.0 %copy-start.18 = (f32[512,512]{1,0:T(8,128)S(1)}, f32[512,512]{1,0:T(8,128)}, u32[]{:S(2)}) copy-start(f32[512,512]{1,0:T(8,128)} %get-tuple-element.43) | copy-start | bytes 3145732

commit v5 on v4

--- a/solution.py
+++ b/solution.py
@@ -45,10 +45,8 @@
     )
     code = jnp.where(member, rank, -1.0).astype(jnp.bfloat16)
     code_u = jnp.where(member_u, rank_u, -1.0)
-    seats = [
-        jnp.sum(jnp.where(code_u == k, target_u, 0), axis=0) for k in range(capacity)
-    ]
-    return code, jnp.stack(seats)
+    seats = lax.broadcasted_iota(jnp.int32, (capacity, 1, 1), 0).astype(jnp.float32)
+    return code, jnp.sum(jnp.where(code_u[None] == seats, target_u[None], 0), axis=1)
 
 
 def owner(queries, targets, block_items, table_ids, counts):
@@ -124,30 +122,30 @@
     return groups
 
 
-def blocks_of(ref):
-    rows, columns = ref.shape
-    return [(c, rows) for c in range(columns // 128)]
+def pieces_of(refs, start, size):
+    row = 0
+    for ref in refs:
+        rows, columns = ref.shape
+        for c in range(columns // 128):
+            low, high = max(start, row), min(start + size, row + rows)
+            if low < high:
+                yield low, high, ref.at[low - row : high - row, c * 128 : (c + 1) * 128]
+            row += rows
+    low = max(start, row)
+    if low < start + size:
+        yield low, start + size, None
 
 
 def reduce_kernel(bits, tiles, big_ref, small_ref, big_out, small_out, acc, out, inbox, full, send, recv):
     me = lax.axis_index("dev")
     mesh = pl.DeviceIdType.MESH
     groups = row_groups(bits, tiles)
-    total = groups[-1][0] + groups[-1][1]
     bit = [(me // (1 << b)) % 2 for b in range(bits)]
     partners = [me + (1 << b) * (1 - 2 * bit[b]) for b in range(bits)]
 
     barrier = pltpu.get_barrier_semaphore()
     for b in range(bits):
         pl.semaphore_signal(barrier, inc=1, device_id=(partners[b],), device_id_type=mesh)
-    row = 0
-    for ref in (big_ref, small_ref):
-        for c, rows in blocks_of(ref):
-            acc[row : row + rows, :] = ref[:, c * 128 : (c + 1) * 128]
-            row += rows
-    if row < total:
-        acc[row:, :] = jnp.zeros((total - row, 128), jnp.float32)
-
     def rows_at(first, count):
         return pl.ds(pl.multiple_of(first, TILE), count)
 
@@ -166,9 +164,13 @@
 
     for s in range(bits):
         for g in range(len(groups)):
-            start, _, order = groups[g]
+            start, size, order = groups[g]
             if s > 0:
                 take(g)
+            else:
+                for low, high, part in pieces_of((big_ref, small_ref), start, size):
+                    blank = jnp.zeros((high - low, 128), jnp.float32)
+                    acc[low:high, :] = blank if part is None else part[...]
             b = order[s]
             half = length[g] // 2
             give = off[g] + (1 - bit[b]) * half
@@ -211,15 +213,13 @@
             started.append(copy)
             off[g] = off[g] - bit[b] * length[g]
             length[g] = length[g] * 2
-    for copy in waiting:
-        copy.wait_recv()
+    for g in range(len(groups)):
+        waiting[g].wait_recv()
+        for low, high, part in pieces_of((big_out, small_out), groups[g][0], groups[g][1]):
+            if part is not None:
+                part[...] = full[low:high, :]
     for copy in started:
         copy.wait_send()
-    row = 0
-    for ref in (big_out, small_out):
-        for c, rows in blocks_of(ref):
-            ref[:, c * 128 : (c + 1) * 128] = full[row : row + rows, :]
-            row += rows
 
 
 def sum_over_devices(big, small):

time: 132 us -> 132 us (level)
  other arithmetic: 15.2 us -> 16.7 us
where the time goes in v5:
time: 132 us; the launch traced here: 131 us
  waiting for transfers between devices  42 us (32%)
  Pallas kernels  32.7 us (25%)
  matrix products  24.3 us (18%)
  other arithmetic  16.7 us (13%)
  starting transfers between devices  11.5 us (9%)
  local copies, waits for them, and re-layouts  2.94 us (2%)
    pallas_call x1, Pallas kernels, sum_over_devices(): pl.pallas_call(functools.partial(reduce_kernel, bits, tiles), out_shape=(...  32.7 us
    all_to_all x1, waiting for transfers between devices, local(): lax.all_to_all(payload, 'dev', split_axis=0, concat_axis=0, tiled=True)  21.7 us
    all_to_all x1, waiting for transfers between devices, local(): lax.all_to_all(back.reshape(devices, rows, width), 'dev', split_axis=0, c...  20.3 us
    all_to_all x1, starting transfers between devices, local(): lax.all_to_all(payload, 'dev', split_axis=0, concat_axis=0, tiled=True)  7.51 us
    reduce_sum x1, other arithmetic, owner(): jnp.sum(jnp.where(table_ids[:, None, :] == which, recip[:, None, :], 0.0)...  5.26 us
    convert_element_type x2, other arithmetic, sum_over_devices(): return tuple((part.astype(jnp.float32) for part in summed))  4.46 us
    all_to_all x1, starting transfers between devices, local(): lax.all_to_all(back.reshape(devices, rows, width), 'dev', split_axis=0, c...  3.97 us
    dot_general x1, matrix products, local(): lax.dot_general(select, returned, (((0,), (0,)), ((), ())), preferred_ele...  3.97 us
  transfers between devices with their start and end apart: 2, of which 2 were waited for; matrix products, arithmetic and copies ran while one was open for 9% of the time, Pallas kernels for 0%

profile of v5, /device:TPU:0, one launch (start us, length us, event | category | flops | bytes accessed | tf_op | source)
XLA Modules:
  0.0 131.2 jit_solution(3561932637017440707)
XLA Ops:
  0.6 0.0 copy-start
  0.7 0.0 copy-start.14
  0.7 1.4 %select_reduce_fusion.2 = s32[4,512]{1,0:T(4,128)S(1)} fusion(s32[512]{0:T(512)} %param.14, s32[4,512]{1,0:T(4,128)} %bitcast.119), kind=kLoop, calls=%fused_computation.10 | loop fusion | flops 3143680 | bytes 18432 | tf_op jit(solution)/shard_map/reduce_sum | solution.py:20
  2.1 0.9 slice_add_fusion.4
  3.0 0.2 eq.221
  3.2 1.1 convolution_select_fusion
  4.3 0.0 copy-done.14
  4.3 0.6 select_select_fusion
  4.9 0.9 select_reduce_fusion.1
  5.8 0.1 reshape.315
  5.9 0.1 copy.79
  6.0 0.1 copy.80
  6.2 0.0 copy-done
  6.2 3.0 %multiply_convert_fusion = (bf16[512,512]{1,0:T(8,128)(2,1)S(1)}, f32[512,512]{1,0:T(8,128)}) fusion(bf16[512,1024]{1,0:T(8,128)(2,1)S(1)} %copy-done, bf16[1024,512]{1,0:T(8,128)(2,1)} %param.10), kind=kOutput, calls=%fused_computation.66 | convolution fusion | flops 538181632 | bytes 3670016 | tf_op jit(solution)/shard_map/dot_general | solution.py:274
  9.1 0.8 fusion.18
  10.0 0.0 copy-start.19
  10.0 0.0 copy-done.6
  10.0 0.1 copy-done.16
  10.2 2.2 %fusion.5 = bf16[4096,128]{1,0:T(8,128)(2,1)S(1)} fusion(bf16[4096]{0:T(1024)(128)(2,1)S(1)} %eq.221, bf16[512,512]{1,0:T(8,128)(2,1)S(1)} %fusion.18, bf16[512,512]{1,0:T(8,128)(2,1)S(1)} %get-tuple-element.34, bf16[512,128]{1,0:T(8,128)(2,1)S(1)} %copy-done.16), kind=kOutput, calls=%fused_computation.8 | convolution fusion | flops 606666752 | bytes 2236416 | tf_op jit(solution)/shard_map/dot_general | solution.py:277
  12.3 0.0 copy-done.19
  12.3 0.0 copy-start.4
  12.3 0.0 copy-start.3
  12.4 1.1 pad_maximum_fusion
  13.4 7.5 %all-to-all-start = ((bf16[32,136,128]{2,1,0:T(8,128)(2,1)}), bf16[32,136,128]{2,1,0:T(8,128)(2,1)S(1)}, u32[]{:S(2)}, u32[]{:S(2)}) async-start(bf16[32,136,128]{2,1,0:T(8,128)(2,1)} %pad_maximum_fusion), calls=%async_computation | async-start | bytes 2228224 | tf_op jit(solution)/shard_map/all_to_all | solution.py:279
  21.0 0.0 copy-done.4
  21.0 0.0 copy-done.3
  21.1 5.3 %select_reduce_fusion = f32[16,128]{1,0:T(8,128)S(1)} fusion(f32[16,4096]{1,0:T(8,128)S(1)} %convert_divide_fusion, s32[16,4096]{1,0:T(8,128)S(1)} %copy-done.3), kind=kLoop, calls=%fused_computation | loop fusion | flops 25163776 | bytes 532480 | tf_op jit(solution)/shard_map/reduce_sum | solution.py:57
  26.3 0.0 copy-start.8
  26.3 0.2 fusion.55
  26.6 0.1 copy.107
  26.7 21.7 %all-to-all-done = bf16[32,136,128]{2,1,0:T(8,128)(2,1)S(1)} async-done(((bf16[32,136,128]{2,1,0:T(8,128)(2,1)}), bf16[32,136,128]{2,1,0:T(8,128)(2,1)S(1)}, u32[]{:S(2)}, u32[]{:S(2)}) %all-to-all-start) | async-done | bytes 1114144 | tf_op jit(solution)/shard_map/all_to_all | solution.py:279
  48.5 0.1 copy.84
  48.6 0.1 copy.87
  48.7 0.1 copy.88
  48.8 0.0 copy-start.5
  48.8 1.4 %select_reduce_fusion.5 = (f32[16,256]{1,0:T(8,128)S(1)}, f32[16,256]{1,0:T(8,128)S(1)}, f32[16,256]{1,0:T(8,128)S(1)}) fusion(s32[16,256]{1,0:T(8,128)S(1)} %broadcast_add_fusion.1, s32[16,256]{1,0:T(8,128)S(1)} %get-tuple-element.15, s32[16,256]{1,0:T(8,128)S(1)} %get-tuple-element.16, bf16[16,96,128]{2,1,0:T(8,128)(2,1)S(1)} %bitcast.102, ...), kind=kOutput, calls=%fused_computation.31 | convolution fusion | flops 104714240 | bytes 507904 | tf_op jit(solution)/shard_map/cql,chl->cqh/dot_general | solution.py:68
  50.2 0.0 copy-done.1
  50.2 0.0 copy-start.10
  50.2 0.0 copy-done.5
  50.2 1.7 %add_reduce_fusion = (f32[16,256]{1,0:T(8,128)S(1)}, f32[16,256,128]{1,2,0:T(8,128)S(1)}) fusion(f32[16,128]{1,0:T(8,128)S(1)} %log.16, bf16[16,128,128]{2,1,0:T(8,128)(2,1)S(1)} %bitcast.93, bf16[32,136,128]{2,1,0:T(8,128)(2,1)} %copy-done.1), kind=kOutput, calls=%fused_computation.26 | convolution fusion | flops 135262208 | bytes 3694592 | tf_op jit(solution)/shard_map/cqe,cie->cqi/dot_general | solution.py:77
  51.9 1.0 select_reduce_fusion.3
  52.9 0.0 copy-start.12
  52.9 1.3 fusion.52
  54.2 0.0 copy-done.8
  54.2 1.3 fusion.16
  55.5 1.3 copy.124
  56.8 4.0 %all-to-all-start.1 = ((bf16[32,128,128]{2,1,0:T(8,128)(2,1)}), bf16[32,128,128]{2,1,0:T(8,128)(2,1)}, u32[]{:S(2)}, u32[]{:S(2)}) async-start(bf16[32,128,128]{2,1,0:T(8,128)(2,1)} %bitcast.89), calls=%async_computation.1 | async-start | bytes 2097152 | tf_op jit(solution)/shard_map/all_to_all | solution.py:294
  60.8 0.1 copy.94
  60.9 0.1 copy.95
  61.0 0.1 copy.86
  61.1 0.1 copy.97
  61.2 0.1 copy.93
  61.3 0.1 copy.96
  61.4 0.2 convert_reduce_fusion
  61.6 0.5 div.73
  62.1 2.2 %fusion.23 = f32[16,128,128]{2,1,0:T(8,128)S(1)} fusion(f32[16,256,128]{1,2,0:T(8,128)S(1)} %get-tuple-element.37, f32[16,256]{1,0:T(8,128)} %copy-done.12, s32[16,256]{1,0:T(8,128)} %copy-done.10, f32[16,256]{1,0:T(8,128)S(1)} %get-tuple-element.36, f32[16,128]{1,0:T(8,128)} %copy-done.8, bf16[32,136,128]{2,1,0:T(8,128)(2,1)} %copy-done.1), kind=kOutput, calls=%fused_computation.47 | convolution fusion | flops 138412032 | bytes 4251648 | tf_op jit(solution)/shard_map/cqi,cqe->cie/dot_general | solution.py:97
  64.4 2.0 %convolution_add_fusion = f32[16,128,128]{2,1,0:T(8,128)} fusion(f32[16,128,128]{2,1,0:T(8,128)S(1)} %fusion.23, f32[16,256,128]{1,2,0:T(8,128)S(1)} %get-tuple-element.37, f32[16,256]{1,0:T(8,128)S(1)} %copy-done.13, s32[16,256]{1,0:T(8,128)S(1)} %copy-done.11, f32[16,256]{1,0:T(8,128)S(1)} %get-tuple-element.36, f32[16,128]{1,0:T(8,128)S(1)} %copy-done.9, ...), kind=kOutput, calls=%fused_computation.38 | convolution fusion | flops 139198464 | bytes 5300224 | tf_op jit(solution)/shard_map/cqi,cqe->cie/dot_general | solution.py:99
  66.4 20.3 %all-to-all-done.1 = bf16[32,128,128]{2,1,0:T(8,128)(2,1)} async-done(((bf16[32,128,128]{2,1,0:T(8,128)(2,1)}), bf16[32,128,128]{2,1,0:T(8,128)(2,1)}, u32[]{:S(2)}, u32[]{:S(2)}) %all-to-all-start.1) | async-done | bytes 1048608 | tf_op jit(solution)/shard_map/all_to_all | solution.py:294
  86.8 4.0 %fusion.19 = bf16[512,128]{1,0:T(8,128)(2,1)S(1)} fusion(bf16[4096,128]{1,0:T(8,128)(2,1)} %bitcast.33, bf16[512,512]{1,0:T(8,128)(2,1)} %copy-done.19, bf16[8]{0:T(256)(128)(2,1)S(1)} %copy-done.15), kind=kOutput, calls=%fused_computation.43 | convolution fusion | flops 539033600 | bytes 1703952 | tf_op jit(solution)/shard_map/dot_general | solution.py:297
  90.7 1.0 fusion.73.small_ref
  91.8 2.3 %convolution_bitcast_fusion.big_ref = f32[1024,512]{1,0:T(8,128)} fusion(bf16[512,1024]{1,0:T(8,128)(2,1)S(1)} %copy-done, bf16[512,128]{1,0:T(8,128)(2,1)S(1)} %fusion.19, bf16[512,128]{1,0:T(8,128)(2,1)S(1)} %copy-done.17, f32[512,512]{1,0:T(8,128)S(1)} %copy-done.18), kind=kOutput, calls=%fused_computation.28 | convolution fusion | flops 606339072 | bytes 4456448 | tf_op jit(solution)/shard_map/dot_general | solution.py:303
  94.1 32.7 %sum_over_devices.1 = (bf16[1024,512]{1,0:T(8,128)(2,1)}, bf16[512,128]{1,0:T(8,128)(2,1)}) custom-call(f32[1024,512]{1,0:T(8,128)} %convolution_bitcast_fusion.big_ref, f32[512,128]{1,0:T(8,128)} %fusion.73.small_ref), custom_call_target="tpu_custom_call" | custom-call | tf_op jit(solution)/shard_map/sum_over_devices/pallas_call | solution.py:231
  126.8 1.6 %convert_element_type.104 = f32[512,128]{1,0:T(8,128)} convert(bf16[512,128]{1,0:T(8,128)(2,1)} %get-tuple-element.7) | non-fusion elementwise | flops 65536 | bytes 393216 | tf_op jit(solution)/shard_map/convert_element_type | solution.py:250
  128.4 2.8 %convert_element_type.103 = f32[1024,512]{1,0:T(8,128)} convert(bf16[1024,512]{1,0:T(8,128)(2,1)} %get-tuple-element.6) | non-fusion elementwise | flops 524288 | bytes 3145728 | tf_op jit(solution)/shard_map/convert_element_type | solution.py:250
  (41 shorter events, 0.4 us)
Async XLA Ops:
  0.6 5.5 %copy-start = (bf16[512,1024]{1,0:T(8,128)(2,1)S(1)}, bf16[512,1024]{1,0:T(8,128)(2,1)}, u32[]{:S(2)}) copy-start(bf16[512,1024]{1,0:T(8,128)(2,1)} %param.9) | copy-start | bytes 3145732
  0.7 3.6 %copy-start.14 = (bf16[8]{0:T(256)(128)(2,1)}, bf16[8]{0:T(256)(128)(2,1)S(1)}, u32[]{:S(2)}) copy-start(bf16[8]{0:T(256)(128)(2,1)S(1)} %iota_convert_fusion.1) | copy-start | bytes 52
  9.1 0.9 copy-start.6
  9.1 1.0 copy-start.16
  10.0 2.3 %copy-start.19 = (bf16[512,512]{1,0:T(8,128)(2,1)}, bf16[512,512]{1,0:T(8,128)(2,1)S(1)}, u32[]{:S(2)}) copy-start(bf16[512,512]{1,0:T(8,128)(2,1)S(1)} %fusion.18) | copy-start | bytes 1572868
  12.3 8.6 %copy-start.4 = (s32[16,4096]{1,0:T(8,128)S(1)}, s32[16,4096]{1,0:T(8,128)}, u32[]{:S(2)}) copy-start(s32[16,4096]{1,0:T(8,128)} %param.16) | copy-start | bytes 786436
  12.3 8.7 %copy-start.3 = (s32[16,4096]{1,0:T(8,128)S(1)}, s32[16,4096]{1,0:T(8,128)}, u32[]{:S(2)}) copy-start(s32[16,4096]{1,0:T(8,128)} %param.15) | copy-start | bytes 786436
  13.4 34.9 %all-to-all-start = ((bf16[32,136,128]{2,1,0:T(8,128)(2,1)}), bf16[32,136,128]{2,1,0:T(8,128)(2,1)S(1)}, u32[]{:S(2)}, u32[]{:S(2)}) async-start(bf16[32,136,128]{2,1,0:T(8,128)(2,1)} %pad_maximum_fusion), calls=%async_computation | async-start | bytes 2228224 | tf_op jit(solution)/shard_map/all_to_all | solution.py:279
  26.3 27.9 %copy-start.8 = (f32[16,128]{1,0:T(8,128)}, f32[16,128]{1,0:T(8,128)S(1)}, u32[]{:S(2)}) copy-start(f32[16,128]{1,0:T(8,128)S(1)} %log.16) | copy-start | bytes 24580
  48.4 1.8 %copy-start.1 = (bf16[32,136,128]{2,1,0:T(8,128)(2,1)}, bf16[32,136,128]{2,1,0:T(8,128)(2,1)S(1)}, u32[]{:S(2)}) copy-start(bf16[32,136,128]{2,1,0:T(8,128)(2,1)S(1)} %all-to-all-done) | copy-start | bytes 3342340
  48.8 1.5 %copy-start.5 = (bf16[2048,128]{1,0:T(8,128)(2,1)S(1)}, bf16[2048,128]{1,0:T(8,128)(2,1)}, u32[]{:S(2)}) copy-start(bf16[2048,128]{1,0:T(8,128)(2,1)} %param.12) | copy-start | bytes 1572868
  50.2 4.0 %copy-start.10 = (s32[16,256]{1,0:T(8,128)}, s32[16,256]{1,0:T(8,128)S(1)}, u32[]{:S(2)}) copy-start(s32[16,256]{1,0:T(8,128)S(1)} %convert_select_fusion) | copy-start | bytes 49156
  52.9 8.1 %copy-start.12 = (f32[16,256]{1,0:T(8,128)}, f32[16,256]{1,0:T(8,128)S(1)}, u32[]{:S(2)}) copy-start(f32[16,256]{1,0:T(8,128)S(1)} %get-tuple-element.9) | copy-start | bytes 49156
  56.8 29.9 %all-to-all-start.1 = ((bf16[32,128,128]{2,1,0:T(8,128)(2,1)}), bf16[32,128,128]{2,1,0:T(8,128)(2,1)}, u32[]{:S(2)}, u32[]{:S(2)}) async-start(bf16[32,128,128]{2,1,0:T(8,128)(2,1)} %bitcast.89), calls=%async_computation.1 | async-start | bytes 2097152 | tf_op jit(solution)/shard_map/all_to_all | solution.py:294
  62.1 2.2 %copy-start.2 = (bf16[32,136,128]{2,1,0:T(8,128)(2,1)S(1)}, bf16[32,136,128]{2,1,0:T(8,128)(2,1)}, u32[]{:S(2)}) copy-start(bf16[32,136,128]{2,1,0:T(8,128)(2,1)} %copy-done.1) | copy-start | bytes 3342340
  62.1 2.3 %copy-start.9 = (f32[16,128]{1,0:T(8,128)S(1)}, f32[16,128]{1,0:T(8,128)}, u32[]{:S(2)}) copy-start(f32[16,128]{1,0:T(8,128)} %copy-done.8) | copy-start | bytes 24580
  62.1 2.3 %copy-start.11 = (s32[16,256]{1,0:T(8,128)S(1)}, s32[16,256]{1,0:T(8,128)}, u32[]{:S(2)}) copy-start(s32[16,256]{1,0:T(8,128)} %copy-done.10) | copy-start | bytes 49156
  62.1 2.3 %copy-start.13 = (f32[16,256]{1,0:T(8,128)S(1)}, f32[16,256]{1,0:T(8,128)}, u32[]{:S(2)}) copy-start(f32[16,256]{1,0:T(8,128)} %copy-done.12) | copy-start | bytes 49156
  64.4 22.3 %copy-start.15 = (bf16[8]{0:T(256)(128)(2,1)S(1)}, bf16[8]{0:T(256)(128)(2,1)}, u32[]{:S(2)}) copy-start(bf16[8]{0:T(256)(128)(2,1)} %copy-done.14) | copy-start | bytes 52
  86.7 4.0 %copy-start.7 = (bf16[512,512]{1,0:T(8,128)(2,1)S(1)}, bf16[512,512]{1,0:T(8,128)(2,1)}, u32[]{:S(2)}) copy-start(bf16[512,512]{1,0:T(8,128)(2,1)} %copy-done.6) | copy-start | bytes 1572868
  86.7 5.0 %copy-start.17 = (bf16[512,128]{1,0:T(8,128)(2,1)S(1)}, bf16[512,128]{1,0:T(8,128)(2,1)}, u32[]{:S(2)}) copy-start(bf16[512,128]{1,0:T(8,128)(2,1)} %param.11) | copy-start | bytes 393220
  86.7 5.0 %copy-start.18 = (f32[512,512]{1,0:T(8,128)S(1)}, f32[512,512]{1,0:T(8,128)}, u32[]{:S(2)}) copy-start(f32[512,512]{1,0:T(8,128)} %get-tuple-element.35) | copy-start | bytes 3145732
